TPU v7x, 512 devices: a whole 4x4x16 slice. The times are simulated.
512 devices in a mesh: clus: 32 (over z, core), grp: 16 (over x, y).
Axes of the slice: x: 4, y: 4, z: 16, core: 2. Of those that a mesh axis runs over, the one named last changes fastest.
Arguments:
- features: bfloat16 [32, 16, 1024, 256], P('clus', 'grp'), may hold values from -6 to 6
- history: bfloat16 [32, 16, 1024, 256], P('clus', 'grp'), may hold values from -6 to 6
- aux_history: bfloat16 [32, 16, 1024, 256], P('clus', 'grp'), may hold values from -0.625 to 0.625
- tile_values: bfloat16 [32, 16, 8, 4, 128, 128], P('clus', 'grp'), may hold values from -0.25 to 0.25
- tile_sources: int32 [32, 16, 8, 4], P('clus', 'grp'), may hold values from 0 to 39, as said below
- send_list: int32 [32, 16, 16, 2], P('clus', 'grp'), may hold values from 0 to 8, as said below
- event_bins: int32 [32, 16, 1024], P('clus', 'grp'), may hold values from 0 to 31
- event_flags: int32 [32, 16, 1024], P('clus', 'grp'), may hold values 0 or 1
- neigh_first: bfloat16 [256, 256], replicated, may hold values from -0.375 to 0.375
- self_first: bfloat16 [256, 256], replicated, may hold values from -0.375 to 0.375
- neigh_second: bfloat16 [256, 256], replicated, may hold values from -0.375 to 0.375
- self_second: bfloat16 [256, 256], replicated, may hold values from -0.375 to 0.375
- hazard_weight: bfloat16 [256, 32], replicated, may hold values from -0.375 to 0.375
Outputs:
- new_history: bfloat16 [32, 16, 1024, 256], P('clus', 'grp')
- grad_hidden: bfloat16 [32, 16, 1024, 256], P('clus', 'grp')
- new_aux: bfloat16 [32, 16, 1024, 256], P('clus', 'grp')
- grad_neigh_first: float32 [256, 256], replicated
- grad_self_first: float32 [256, 256], replicated
- grad_neigh_second: float32 [256, 256], replicated
- grad_self_second: float32 [256, 256], replicated
- grad_hazard: float32 [256, 32], replicated
- loss: float32 [], replicated
Inputs may be any that keep to these rules, and one draw needn't show every extreme that they name: `send_list`: entry [c, g, p, s] names the block of device (c, g) sent to device (c, p) in slot s, or 8 for an empty slot; live slots come first in a list; a device's list to itself is empty; every other list has one or two live slots, and every device has at least one full list and at least one list with a single live slot. `tile_sources`: indexes the device's source table; never an empty slot; every live received slot is read by some tile.
All inputs are finite; a program needn't handle non-finite values. No bound on the sum of `event_flags` on one device may be relied on, other than what follows from the above.
Results may differ from a plain program's by a relative error of at most 0.014.
Values may be sent and summed in bfloat16 or wider, within the bound.
A program may use at most 64 MiB of HBM per device.

v0:
```python
import jax
import jax.numpy as jnp
from jax import lax
from jax.sharding import PartitionSpec as P


def silu_slope(preact):
    logistic = jax.nn.sigmoid(preact)
    return logistic * (1.0 + preact * (1.0 - logistic))


def aggregate(source_table, sources, tile_vals):
    picked = source_table[sources]
    return jnp.einsum("bkij,bkjd->bid", tile_vals, picked, preferred_element_type=jnp.float32)


def spread_back(tile_vals, sources, grad_blocks, table_size):
    contribution = jnp.einsum(
        "bkij,bid->bkjd", tile_vals, grad_blocks, preferred_element_type=jnp.float32
    )
    flattened = contribution.reshape((-1,) + contribution.shape[2:])
    return jax.ops.segment_sum(flattened, sources.reshape(-1), num_segments=table_size)


def transpose_dot(former, latter):
    return lax.dot_general(
        former, latter, (((0,), (0,)), ((), ())), preferred_element_type=jnp.float32
    )


def dot_by_transpose(former, latter):
    return lax.dot_general(
        former, latter, (((1,), (1,)), ((), ())), preferred_element_type=jnp.float32
    )


def shards(
    features,
    history,
    aux_history,
    tile_values,
    tile_sources,
    send_list,
    event_bins,
    event_flags,
    neigh_first,
    self_first,
    neigh_second,
    self_second,
    hazard_weight,
):
    tile_vals = tile_values[0, 0]
    sources = tile_sources[0, 0]
    routing = send_list[0, 0]
    block_count = tile_vals.shape[0]
    block_rows = tile_vals.shape[2]
    feat_width = features.shape[3]
    peer_count = lax.axis_size("grp")
    slot_count = routing.shape[1]
    node_rows = block_count * block_rows
    row_scale = 1.0 / (node_rows * peer_count)
    table_size = block_count + peer_count * slot_count
    own_rows = features[0, 0]
    past_rows = history[0, 0]
    selector = (
        routing.reshape(-1)[:, None] == jnp.arange(block_count, dtype=jnp.int32)[None, :]
    ).astype(jnp.bfloat16)

    def outgoing(values):
        flattened = values.reshape(block_count, block_rows * feat_width)
        packed = jnp.dot(selector, flattened, preferred_element_type=jnp.float32)
        return packed.astype(jnp.bfloat16).reshape(peer_count, slot_count, block_rows, feat_width)

    def table_of(values, incoming):
        own = values.reshape(block_count, block_rows, feat_width)
        return jnp.concatenate(
            [own, incoming.reshape(peer_count * slot_count, block_rows, feat_width)], axis=0
        )

    feat_in = lax.all_to_all(outgoing(own_rows), "grp", split_axis=0, concat_axis=0, tiled=True)
    agg_first = (
        aggregate(table_of(own_rows, feat_in), sources, tile_vals)
        .astype(jnp.bfloat16)
        .reshape(node_rows, feat_width)
    )
    pre_first = jnp.dot(agg_first, neigh_first, preferred_element_type=jnp.float32) + jnp.dot(
        own_rows, self_first, preferred_element_type=jnp.float32
    )
    hidden_first = jax.nn.silu(pre_first).astype(jnp.bfloat16)
    past_in = lax.all_to_all(outgoing(past_rows), "grp", split_axis=0, concat_axis=0, tiled=True)
    agg_second = (
        aggregate(table_of(hidden_first, past_in), sources, tile_vals)
        .astype(jnp.bfloat16)
        .reshape(node_rows, feat_width)
    )
    pre_second = jnp.dot(agg_second, neigh_second, preferred_element_type=jnp.float32) + jnp.dot(
        hidden_first, self_second, preferred_element_type=jnp.float32
    )
    hidden_second = jax.nn.silu(pre_second).astype(jnp.bfloat16)
    logits = jnp.dot(hidden_second, hazard_weight, preferred_element_type=jnp.float32)
    bins_col = event_bins[0, 0][:, None]
    flag_col = event_flags[0, 0][:, None].astype(jnp.float32)
    step_row = jnp.arange(logits.shape[1], dtype=jnp.int32)[None, :]
    counted = step_row <= bins_col
    at_event = (step_row == bins_col).astype(jnp.float32)
    node_loss = jnp.sum(jnp.where(counted, jax.nn.softplus(logits), 0.0), axis=1) - flag_col[
        :, 0
    ] * jnp.sum(at_event * logits, axis=1)
    part_loss = jnp.sum(node_loss) * row_scale
    grad_logits = (jnp.where(counted, jax.nn.sigmoid(logits), 0.0) - flag_col * at_event).astype(
        jnp.bfloat16
    )
    grad_hazard = transpose_dot(hidden_second, grad_logits) * row_scale
    grad_pre_second = (
        dot_by_transpose(grad_logits, hazard_weight) * silu_slope(pre_second)
    ).astype(jnp.bfloat16)
    grad_neigh_second = transpose_dot(agg_second, grad_pre_second) * row_scale
    grad_self_second = transpose_dot(hidden_first, grad_pre_second) * row_scale
    grad_agg = dot_by_transpose(grad_pre_second, neigh_second).astype(jnp.bfloat16)
    grad_table = spread_back(
        tile_vals, sources, grad_agg.reshape(block_count, block_rows, feat_width), table_size
    )
    sent_back = (
        grad_table[block_count:]
        .astype(jnp.bfloat16)
        .reshape(peer_count, slot_count, block_rows, feat_width)
    )
    came_back = lax.all_to_all(sent_back, "grp", split_axis=0, concat_axis=0, tiled=True)
    aux_sum = transpose_dot(
        selector, came_back.reshape(peer_count * slot_count, block_rows * feat_width)
    )
    new_aux = aux_sum.astype(jnp.bfloat16).reshape(node_rows, feat_width)
    grad_total = (
        grad_table[:block_count].reshape(node_rows, feat_width)
        + dot_by_transpose(grad_pre_second, self_second)
        + aux_history[0, 0].astype(jnp.float32)
    )
    grad_hidden = grad_total.astype(jnp.bfloat16)
    grad_pre_first = (grad_total * silu_slope(pre_first)).astype(jnp.bfloat16)
    grad_neigh_first = transpose_dot(agg_first, grad_pre_first) * row_scale
    grad_self_first = transpose_dot(own_rows, grad_pre_first) * row_scale
    (
        grad_neigh_first,
        grad_self_first,
        grad_neigh_second,
        grad_self_second,
        grad_hazard,
        part_loss,
    ) = lax.psum(
        (
            grad_neigh_first,
            grad_self_first,
            grad_neigh_second,
            grad_self_second,
            grad_hazard,
            part_loss,
        ),
        ("clus", "grp"),
    )
    return (
        hidden_first[None, None],
        grad_hidden[None, None],
        new_aux[None, None],
        grad_neigh_first,
        grad_self_first,
        grad_neigh_second,
        grad_self_second,
        grad_hazard,
        part_loss,
    )


def solution(mesh):
    in_specs = (
        P("clus", "grp", None, None),
        P("clus", "grp", None, None),
        P("clus", "grp", None, None),
        P("clus", "grp", None, None, None, None),
        P("clus", "grp", None, None),
        P("clus", "grp", None, None),
        P("clus", "grp", None),
        P("clus", "grp", None),
        P(),
        P(),
        P(),
        P(),
        P(),
    )
    out_specs = (
        P("clus", "grp", None, None),
        P("clus", "grp", None, None),
        P("clus", "grp", None, None),
        P(),
        P(),
        P(),
        P(),
        P(),
        P(),
    )
    return jax.shard_map(shards, mesh=mesh, in_specs=in_specs, out_specs=out_specs, check_vma=False)
```

profile of v0, /device:TPU:1, one launch (start us, length us, event | category | flops | bytes accessed | tf_op | source)
XLA Modules:
  0.0 616.9 jit_solution(14401469925907181316)
XLA Ops:
  7.2 0.0 copy-start
  7.2 0.8 copy.28
  8.0 0.1 eq.10
  8.1 1.3 reshape_squeeze.10
  9.4 0.7 convolution_convert_fusion.1
  10.2 1.8 copy.39
  12.0 7.6 %all-to-all-start = ((bf16[16,2,128,256]{3,2,1,0:T(8,128)(2,1)}), bf16[16,2,128,256]{3,2,1,0:T(8,128)(2,1)S(1)}, u32[]{:S(2)}, u32[]{:S(2)}) async-start(bf16[16,2,128,256]{3,2,1,0:T(8,128)(2,1)} %bitcast.113), calls=%async_computation | async-start | bytes 4194304 | tf_op jit(solution)/shard_map/all_to_all | solution.py:80
  19.6 2.1 reshape_squeeze.11
  21.7 1.8 convolution_convert_fusion
  23.4 1.9 copy.40
  25.3 19.6 %all-to-all-done = bf16[16,2,128,256]{3,2,1,0:T(8,128)(2,1)S(1)} async-done(((bf16[16,2,128,256]{3,2,1,0:T(8,128)(2,1)}), bf16[16,2,128,256]{3,2,1,0:T(8,128)(2,1)S(1)}, u32[]{:S(2)}, u32[]{:S(2)}) %all-to-all-start) | async-done | bytes 2097184 | tf_op jit(solution)/shard_map/all_to_all | solution.py:80
  44.9 6.7 %all-to-all-start.1 = ((bf16[16,2,128,256]{3,2,1,0:T(8,128)(2,1)}), bf16[16,2,128,256]{3,2,1,0:T(8,128)(2,1)}, u32[]{:S(2)}, u32[]{:S(2)}) async-start(bf16[16,2,128,256]{3,2,1,0:T(8,128)(2,1)} %bitcast.46), calls=%async_computation.1 | async-start | bytes 4194304 | tf_op jit(solution)/shard_map/all_to_all | solution.py:90
  51.6 0.1 copy.30
  51.7 0.1 copy.29
  51.8 0.1 reshape.110
  51.9 0.1 reshape.126
  51.9 2.8 pad_maximum_fusion
  54.7 2.4 gather_fusion
  57.2 0.0 copy-start.20
  57.2 0.5 fusion.2
  57.7 0.8 copy-done.3
  58.5 0.3 fusion.16
  58.8 1.4 multiply_convert_fusion.2
  60.2 16.6 %all-to-all-done.1 = bf16[16,2,128,256]{3,2,1,0:T(8,128)(2,1)} async-done(((bf16[16,2,128,256]{3,2,1,0:T(8,128)(2,1)}), bf16[16,2,128,256]{3,2,1,0:T(8,128)(2,1)}, u32[]{:S(2)}, u32[]{:S(2)}) %all-to-all-start.1) | async-done | bytes 2097184 | tf_op jit(solution)/shard_map/all_to_all | solution.py:90
  76.7 3.3 pad_maximum_fusion.1
  80.1 2.4 gather_fusion.1
  82.5 0.0 copy-start.8
  82.5 0.0 copy-start.21
  82.5 0.5 fusion.3
  83.1 0.0 copy-start.5
  83.1 0.3 copy-done.12
  83.4 0.3 fusion.17
  83.7 0.0 copy-start.22
  83.8 0.5 multiply_convert_fusion.1
  84.2 0.2 copy-done.22
  84.5 0.3 select_reduce_fusion
  84.8 0.5 fusion.1
  85.3 0.8 copy-done.10
  86.1 0.3 convolution_convert_fusion.3
  86.4 2.7 fusion.5
  89.1 5.7 copy.32
  94.8 3.0 broadcast_in_dim.19
  97.8 10.1 %scatter_fusion = f32[40,128,256]{2,1,0:T(8,128)} fusion(f32[40,128,256]{2,1,0:T(8,128)} %broadcast_in_dim.19, s32[32]{0:T(128)S(1)} %reshape.126, f32[32,128,256]{2,1,0:T(8,128)} %copy.32), kind=kCustom, calls=%fused_computation.2 | custom fusion | flops 1048576 | bytes 12583040 | tf_op jit(solution)/shard_map/scatter-add | solution.py:22
  107.9 3.8 slice.16
  111.7 7.0 %all-to-all-start.2 = ((bf16[16,2,128,256]{3,2,1,0:T(8,128)(2,1)}), bf16[16,2,128,256]{3,2,1,0:T(8,128)(2,1)S(1)}, u32[]{:S(2)}, u32[]{:S(2)}) async-start(bf16[16,2,128,256]{3,2,1,0:T(8,128)(2,1)} %bitcast.111), calls=%async_computation.2 | async-start | bytes 4194304 | tf_op jit(solution)/shard_map/all_to_all | solution.py:128
  118.7 0.2 all-reduce.4.cloned.1.call-start
  119.0 1.5 slice.13
  120.5 1.0 convolution_multiply_fusion.2
  121.5 1.0 convolution_multiply_fusion.1
  122.6 1.4 multiply_convert_fusion
  124.0 1.0 convolution_multiply_fusion.4
  125.0 1.0 fusion.4
  126.1 0.0 all-reduce.4.cloned.1.call-update
  126.1 0.6 subtract_reduce_fusion
  127.4 1.3 convolution_multiply_fusion.5
  128.6 119.8 %all-reduce = (f32[256,32]{0,1:T(8,128)}, f32[]{:T(128)}) all-reduce(f32[256,32]{0,1:T(8,128)S(1)} %convolution_multiply_fusion.5, f32[]{:T(128)S(6)} %mul.82), channel_id=1, replica_groups=mesh['clus'=32,'grp'=16] {'clus','grp'}, use_global_device_ids=true, to_apply=%region_5.6 | all-reduce | flops 8193 | bytes 65544 | tf_op jit(solution)/shard_map/psum | solution.py:149
  248.4 355.0 %all-reduce.4.cloned.1.call-done = (f32[256,256]{1,0:T(8,128)}, f32[256,256]{0,1:T(8,128)}, f32[256,256]{1,0:T(8,128)}, f32[256,256]{1,0:T(8,128)}) async-done(((f32[256,256]{1,0:T(8,128)}, f32[256,256]{0,1:T(8,128)}, f32[256,256]{1,0:T(8,128)}, f32[256,256]{1,0:T(8,128)}), (f32[256,256]{1,0:T(8,128)}, f32[256,256]{0,1:T(8,128)}, f32[256,256]{1,0:T(8,128)}, ...) | async-done | bytes 1048592 | tf_op jit(solution)/shard_map/psum | solution.py:149
  603.4 1.8 copy.33
  605.2 1.2 copy.41
  606.4 0.5 convolution_convert_fusion.2
  606.9 1.0 broadcast_in_dim_reshape.3
  607.9 0.7 copy.47
  608.6 0.7 copy.48
  609.4 0.7 copy.49
  (46 shorter events, 0.1 us)
Async XLA Ops:
  7.2 50.0 %copy-start = (bf16[1,1,8,4,128,128]{5,4,3,2,1,0:T(8,128)(2,1)S(1)}, bf16[1,1,8,4,128,128]{5,4,3,2,1,0:T(8,128)(2,1)}, u32[]{:S(2)}) copy-start(bf16[1,1,8,4,128,128]{5,4,3,2,1,0:T(8,128)(2,1)} %param.16) | copy-start | bytes 3145732
  12.0 32.9 %all-to-all-start = ((bf16[16,2,128,256]{3,2,1,0:T(8,128)(2,1)}), bf16[16,2,128,256]{3,2,1,0:T(8,128)(2,1)S(1)}, u32[]{:S(2)}, u32[]{:S(2)}) async-start(bf16[16,2,128,256]{3,2,1,0:T(8,128)(2,1)} %bitcast.113), calls=%async_computation | async-start | bytes 4194304 | tf_op jit(solution)/shard_map/all_to_all | solution.py:80
  44.9 6.7 %copy-start.17 = (s32[1,1,8,4]{2,3,1,0:T(4,128)S(1)}, s32[1,1,8,4]{2,3,1,0:T(4,128)}, u32[]{:S(2)}) copy-start(s32[1,1,8,4]{2,3,1,0:T(4,128)} %param.17) | copy-start | bytes 388
  44.9 6.9 %copy-start.18 = (s32[1,1,1024]{2,1,0:T(1,128)S(1)}, s32[1,1,1024]{2,1,0:T(1,128)}, u32[]{:S(2)}) copy-start(s32[1,1,1024]{2,1,0:T(1,128)} %param.20) | copy-start | bytes 12292
  44.9 31.8 %all-to-all-start.1 = ((bf16[16,2,128,256]{3,2,1,0:T(8,128)(2,1)}), bf16[16,2,128,256]{3,2,1,0:T(8,128)(2,1)}, u32[]{:S(2)}, u32[]{:S(2)}) async-start(bf16[16,2,128,256]{3,2,1,0:T(8,128)(2,1)} %bitcast.46), calls=%async_computation.1 | async-start | bytes 4194304 | tf_op jit(solution)/shard_map/all_to_all | solution.py:90
  57.2 1.4 copy-start.16
  57.2 1.6 copy-start.1
  57.2 1.6 copy-start.20
  57.7 0.8 copy-start.3
  60.2 16.6 %copy-start.7 = (bf16[1024,256]{1,0:T(8,128)(2,1)}, bf16[1024,256]{1,0:T(8,128)(2,1)S(1)}, u32[]{:S(2)}) copy-start(bf16[1024,256]{1,0:T(8,128)(2,1)S(1)} %get-tuple-element.37) | copy-start | bytes 1572868
  82.5 0.9 copy-start.12
  82.5 1.2 copy-start.8
  82.5 1.2 copy-start.21
  83.1 1.2 copy-start.5
  83.7 0.7 copy-start.22
  83.7 0.7 copy-start.23
  84.2 1.1 copy-start.24
  85.3 0.8 copy-start.10
  111.7 493.5 %all-to-all-start.2 = ((bf16[16,2,128,256]{3,2,1,0:T(8,128)(2,1)}), bf16[16,2,128,256]{3,2,1,0:T(8,128)(2,1)S(1)}, u32[]{:S(2)}, u32[]{:S(2)}) async-start(bf16[16,2,128,256]{3,2,1,0:T(8,128)(2,1)} %bitcast.111), calls=%async_computation.2 | async-start | bytes 4194304 | tf_op jit(solution)/shard_map/all_to_all | solution.py:128
  118.7 484.7 %all-reduce.4.cloned.1.call-start = ((), (), s32[]{:S(2)}) async-start(), calls=%async_computation.3 | async-start | bytes 2097152 | tf_op jit(solution)/shard_map/psum | solution.py:149
  118.9 1.5 copy-start.6
  119.0 1.5 copy-start.11
  119.0 2.6 copy-start.9
  119.0 3.6 copy-start.19
  119.0 3.6 copy-start.25
  122.6 1.4 copy-start.4
  122.6 2.4 copy-start.2
  606.3 1.6 copy-start.15
  606.4 2.3 copy-start.14
  606.4 3.0 copy-start.13
Sparse Core Ops, SparseCore 0:
  126.2 477.0 all-reduce.3
where the time goes:
time: 618 us; the launch traced here: 617 us
  waiting for transfers between devices  391 us (63%)
  blocking collectives  120 us (19%)
  local copies, waits for them, and re-layouts  35.5 us (6%)
  starting transfers between devices  21.5 us (3%)
  matrix products  17.1 us (3%)
  other arithmetic  16.8 us (3%)
  between operations  15.1 us (2%)
    psum x1, waiting for transfers between devices, shards(): lax.psum((grad_neigh_first, grad_self_first, grad_neigh_second, grad_self...  355 us
    psum x1, blocking collectives, shards(): lax.psum((grad_neigh_first, grad_self_first, grad_neigh_second, grad_self...  120 us
    all_to_all x1, waiting for transfers between devices, shards(): lax.all_to_all(outgoing(own_rows), 'grp', split_axis=0, concat_axis=0, ti...  19.6 us
    all_to_all x1, waiting for transfers between devices, shards(): lax.all_to_all(outgoing(past_rows), 'grp', split_axis=0, concat_axis=0, t...  16.6 us
  transfers between devices with their start and end apart: 4, of which 3 were waited for; matrix products, arithmetic and copies ran while one was open for 4% of the time, Pallas kernels for 0%

commit v1 on v0

--- a/solution.py
+++ b/solution.py
@@ -1,7 +1,204 @@
+import functools
+
 import jax
 import jax.numpy as jnp
 from jax import lax
+from jax.experimental import pallas as pl
+from jax.experimental.pallas import tpu as pltpu
 from jax.sharding import PartitionSpec as P
+
+MESH = pl.DeviceIdType.MESH
+PIECE = 40
+UNITS = 10
+
+
+def owner(unit, depth):
+    return (unit * depth) // UNITS
+
+
+def reduce_kernel(groups, depth, x_ref, o_ref, acc, from_core, from_grp, mine, from_z, done,
+                  core_sem, grp_send, grp_recv, z_send, z_recv, zb_send, zb_recv,
+                  back_send, back_recv, fwd_send, fwd_recv):
+    clus = lax.axis_index("clus")
+    g = lax.axis_index("grp")
+    core = lax.rem(clus, 2)
+    z = clus // 2
+    sibling = clus + 1 - 2 * core
+
+    def grp_peer(d):
+        return lax.rem(g + d, groups)
+
+    def z_peer(d):
+        return lax.rem(z + d, depth)
+
+    barrier = pltpu.get_barrier_semaphore()
+    pl.semaphore_signal(barrier, inc=1, device_id={"clus": sibling}, device_id_type=MESH)
+
+    @pl.loop(1, groups)
+    def _(d):
+        pl.semaphore_signal(barrier, inc=1, device_id={"grp": grp_peer(d)}, device_id_type=MESH)
+
+    @pl.loop(1, depth)
+    def _(d):
+        pl.semaphore_signal(
+            barrier, inc=1, device_id={"clus": z_peer(d) * 2 + core}, device_id_type=MESH
+        )
+
+    pl.semaphore_wait(barrier, groups + depth - 1)
+
+    swap = pltpu.make_async_remote_copy(
+        src_ref=x_ref.at[1 - core], dst_ref=from_core, send_sem=core_sem.at[0],
+        recv_sem=core_sem.at[1], device_id={"clus": sibling}, device_id_type=MESH,
+    )
+    swap.start()
+    swap.wait()
+    acc[...] = x_ref[core] + from_core[...]
+
+    def spread(d):
+        p = grp_peer(d)
+        return pltpu.make_async_remote_copy(
+            src_ref=acc.at[p], dst_ref=from_grp.at[g], send_sem=grp_send.at[p],
+            recv_sem=grp_recv.at[g], device_id={"grp": p}, device_id_type=MESH,
+        )
+
+    def arrived(d):
+        p = grp_peer(d)
+        return pltpu.make_async_remote_copy(
+            src_ref=acc.at[p], dst_ref=from_grp.at[p], send_sem=grp_send.at[p],
+            recv_sem=grp_recv.at[p], device_id={"grp": p}, device_id_type=MESH,
+        )
+
+    @pl.loop(1, groups)
+    def _(d):
+        spread(d).start()
+
+    mine[...] = acc[g]
+
+    @pl.loop(1, groups)
+    def _(d):
+        arrived(d).wait_recv()
+        mine[...] += from_grp[grp_peer(d)]
+
+    @pl.loop(1, groups)
+    def _(d):
+        spread(d).wait_send()
+
+    def unit_of(ref, u):
+        return ref.at[pl.ds(8 * (u // 2), 8), pl.ds(128 * (u % 2), 128)]
+
+    def to_owner(u):
+        return pltpu.make_async_remote_copy(
+            src_ref=unit_of(mine, u), dst_ref=from_z.at[z], send_sem=z_send.at[u],
+            recv_sem=z_recv.at[z], device_id={"clus": owner(u, depth) * 2 + core},
+            device_id_type=MESH,
+        )
+
+    for u in range(UNITS):
+        @pl.when(z != owner(u, depth))
+        def _():
+            to_owner(u).start()
+
+    def share(u, d):
+        q = z_peer(d)
+        return pltpu.make_async_remote_copy(
+            src_ref=unit_of(done, u), dst_ref=unit_of(done, u), send_sem=zb_send.at[q],
+            recv_sem=zb_recv.at[u], device_id={"clus": q * 2 + core}, device_id_type=MESH,
+        )
+
+    for u in range(UNITS):
+        @pl.when(z == owner(u, depth))
+        def _():
+            def gather(d, total):
+                q = z_peer(d)
+                pltpu.make_async_remote_copy(
+                    src_ref=unit_of(mine, u), dst_ref=from_z.at[q], send_sem=z_send.at[u],
+                    recv_sem=z_recv.at[q], device_id={"clus": q * 2 + core}, device_id_type=MESH,
+                ).wait_recv()
+                return total + from_z[q]
+
+            unit_of(done, u)[...] = lax.fori_loop(1, depth, gather, unit_of(mine, u)[...])
+
+            @pl.loop(1, depth)
+            def _(d):
+                share(u, d).start()
+
+    for u in range(UNITS):
+        @pl.when(z != owner(u, depth))
+        def _():
+            to_owner(u).wait_send()
+            share(u, 1).wait_recv()
+
+    def publish(d):
+        p = grp_peer(d)
+        return pltpu.make_async_remote_copy(
+            src_ref=done, dst_ref=o_ref.at[core, g], send_sem=back_send.at[p],
+            recv_sem=back_recv.at[g], device_id={"grp": p}, device_id_type=MESH,
+        )
+
+    def forward(half, p):
+        return pltpu.make_async_remote_copy(
+            src_ref=o_ref.at[half, p], dst_ref=o_ref.at[half, p], send_sem=fwd_send.at[p],
+            recv_sem=fwd_recv.at[p], device_id={"clus": sibling}, device_id_type=MESH,
+        )
+
+    @pl.loop(1, groups)
+    def _(d):
+        publish(d).start()
+
+    o_ref[core, g] = done[...]
+    forward(core, g).start()
+
+    @pl.loop(1, groups)
+    def _(d):
+        p = grp_peer(d)
+        pltpu.make_async_remote_copy(
+            src_ref=done, dst_ref=o_ref.at[core, p], send_sem=back_send.at[p],
+            recv_sem=back_recv.at[p], device_id={"grp": p}, device_id_type=MESH,
+        ).wait_recv()
+        forward(core, p).start()
+
+    @pl.loop(0, groups)
+    def _(p):
+        forward(core, p).wait_send()
+        forward(1 - core, p).wait_recv()
+
+    @pl.loop(1, groups)
+    def _(d):
+        publish(d).wait_send()
+
+    for u in range(UNITS):
+        @pl.when(z == owner(u, depth))
+        def _():
+            @pl.loop(1, depth)
+            def _(d):
+                share(u, d).wait_send()
+
+
+def reduce_all(packed):
+    groups = packed.shape[1]
+    depth = lax.axis_size("clus") // 2
+    width = packed.shape[3]
+    dma = pltpu.SemaphoreType.DMA
+    return pl.pallas_call(
+        functools.partial(reduce_kernel, groups, depth),
+        out_shape=jax.ShapeDtypeStruct(packed.shape, jnp.float32),
+        in_specs=[pl.BlockSpec(memory_space=pltpu.VMEM)],
+        out_specs=pl.BlockSpec(memory_space=pltpu.VMEM),
+        scratch_shapes=[
+            pltpu.VMEM((groups, PIECE, width), jnp.float32),
+            pltpu.VMEM((groups, PIECE, width), jnp.float32),
+            pltpu.VMEM((groups, PIECE, width), jnp.float32),
+            pltpu.VMEM((PIECE, width), jnp.float32),
+            pltpu.VMEM((depth, 8, 128), jnp.float32),
+            pltpu.VMEM((PIECE, width), jnp.float32),
+            dma((2,)), dma((groups,)), dma((groups,)), dma((UNITS,)), dma((depth,)),
+            dma((depth,)), dma((UNITS,)), dma((groups,)), dma((groups,)), dma((groups,)),
+            dma((groups,)),
+        ],
+        compiler_params=pltpu.CompilerParams(
+            collective_id=0, has_side_effects=True, vmem_limit_bytes=32 << 20
+        ),
+    )(packed)
 
 
 def silu_slope(preact):
@@ -139,24 +336,23 @@
     grad_pre_first = (grad_total * silu_slope(pre_first)).astype(jnp.bfloat16)
     grad_neigh_first = transpose_dot(agg_first, grad_pre_first) * row_scale
     grad_self_first = transpose_dot(own_rows, grad_pre_first) * row_scale
-    (
-        grad_neigh_first,
-        grad_self_first,
-        grad_neigh_second,
-        grad_self_second,
-        grad_hazard,
-        part_loss,
-    ) = lax.psum(
-        (
-            grad_neigh_first,
-            grad_self_first,
-            grad_neigh_second,
-            grad_self_second,
-            grad_hazard,
-            part_loss,
-        ),
-        ("clus", "grp"),
-    )
+    halves = lambda first, second: jnp.stack([first, second]).reshape(2, 16, 16, feat_width)
+    loss_row = jnp.broadcast_to(part_loss, (2, 16, 1, feat_width))
+    packed = jnp.concatenate(
+        [
+            halves(grad_neigh_first, grad_self_first),
+            halves(grad_neigh_second, grad_self_second),
+            grad_hazard.reshape(2, 16, 1, feat_width),
+            loss_row,
+            jnp.zeros((2, 16, 6, feat_width), jnp.float32),
+        ],
+        axis=2,
+    )
+    summed = reduce_all(packed)
+    grad_neigh_first, grad_self_first = summed[:, :, 0:16].reshape(2, feat_width, feat_width)
+    grad_neigh_second, grad_self_second = summed[:, :, 16:32].reshape(2, feat_width, feat_width)
+    grad_hazard = summed[:, :, 32].reshape(grad_hazard.shape)
+    part_loss = summed[0, 0, 33, 0]
     return (
         hidden_first[None, None],
         grad_hidden[None, None],

time: 618 us -> 194 us (0.31)
  waiting for transfers between devices: 391 us -> 36.2 us
  blocking collectives: 120 us -> 0 us
  Pallas kernels: 0 us -> 59 us
  between operations: 15.1 us -> 1.77 us
    psum x1 -> x0, waiting for transfers between devices: 355 us -> none  [shards(): lax.psum((grad_neigh_first, grad_self_first, grad_neigh_second, grad_self...]
    psum x1 -> x0, blocking collectives: 120 us -> none  [shards(): lax.psum((grad_neigh_first, grad_self_first, grad_neigh_second, grad_self...]
    pallas_call x0 -> x1, Pallas kernels: none -> 59 us  [reduce_all(): pl.pallas_call(functools.partial(reduce_kernel, groups, depth), out_shape...]
  transfers between devices with their start and end apart: 4 -> 3, of which waited for: 3 -> 2; matrix products, arithmetic and copies ran while one was open for 4% -> 14% of each run, Pallas kernels for 0% -> 31%
where the time goes in v1:
time: 194 us; the launch traced here: 193 us
  Pallas kernels  59 us (30%)
  local copies, waits for them, and re-layouts  41.2 us (21%)
  waiting for transfers between devices  36.2 us (19%)
  starting transfers between devices  21.5 us (11%)
  other arithmetic  16.8 us (9%)
  matrix products  16.5 us (9%)
    pallas_call x1, Pallas kernels, reduce_all(): pl.pallas_call(functools.partial(reduce_kernel, groups, depth), out_shape...  59 us
    all_to_all x1, waiting for transfers between devices, shards(): lax.all_to_all(outgoing(own_rows), 'grp', split_axis=0, concat_axis=0, ti...  19.6 us
    all_to_all x1, waiting for transfers between devices, shards(): lax.all_to_all(outgoing(past_rows), 'grp', split_axis=0, concat_axis=0, t...  16.6 us
    unnamed x54, local copies, waits for them, and re-layouts  11.6 us
    scatter-add x1, other arithmetic, spread_back(): jax.ops.segment_sum(flattened, sources.reshape(-1), num_segments=table_size)  10.1 us
    all_to_all x1, starting transfers between devices, shards(): lax.all_to_all(outgoing(own_rows), 'grp', split_axis=0, concat_axis=0, ti...  7.58 us
    all_to_all x1, starting transfers between devices, shards(): lax.all_to_all(sent_back, 'grp', split_axis=0, concat_axis=0, tiled=True)  7.25 us
    all_to_all x1, starting transfers between devices, shards(): lax.all_to_all(outgoing(past_rows), 'grp', split_axis=0, concat_axis=0, t...  6.67 us
  transfers between devices with their start and end apart: 3, of which 2 were waited for; matrix products, arithmetic and copies ran while one was open for 14% of the time, Pallas kernels for 31%

profile of v1, /device:TPU:1, one launch (start us, length us, event | category | flops | bytes accessed | tf_op | source)
XLA Modules:
  0.0 193.0 jit_solution(3989698859514573222)
XLA Ops:
  0.7 0.8 copy.31
  1.5 0.1 eq.10
  1.6 1.3 reshape_squeeze.13
  2.9 0.7 convolution_convert_fusion.1
  3.6 1.8 copy.47
  5.5 7.6 %all-to-all-start = ((bf16[16,2,128,256]{3,2,1,0:T(8,128)(2,1)}), bf16[16,2,128,256]{3,2,1,0:T(8,128)(2,1)S(1)}, u32[]{:S(2)}, u32[]{:S(2)}) async-start(bf16[16,2,128,256]{3,2,1,0:T(8,128)(2,1)} %bitcast.120), calls=%async_computation | async-start | bytes 4194304 | tf_op jit(solution)/shard_map/all_to_all | solution.py:277
  13.0 2.1 %reshape_squeeze.14 = bf16[8,32768]{1,0:T(8,128)(2,1)} reshape(bf16[1,1,1024,256]{3,2,1,0:T(8,128)(2,1)} %param.14) | data formatting | bytes 1048576 | tf_op jit(solution)/shard_map/reshape;squeeze | solution.py:267
  15.1 1.8 convolution_convert_fusion
  16.9 1.9 copy.48
  18.8 19.6 %all-to-all-done = bf16[16,2,128,256]{3,2,1,0:T(8,128)(2,1)S(1)} async-done(((bf16[16,2,128,256]{3,2,1,0:T(8,128)(2,1)}), bf16[16,2,128,256]{3,2,1,0:T(8,128)(2,1)S(1)}, u32[]{:S(2)}, u32[]{:S(2)}) %all-to-all-start) | async-done | bytes 2097184 | tf_op jit(solution)/shard_map/all_to_all | solution.py:277
  38.4 6.7 %all-to-all-start.1 = ((bf16[16,2,128,256]{3,2,1,0:T(8,128)(2,1)}), bf16[16,2,128,256]{3,2,1,0:T(8,128)(2,1)}, u32[]{:S(2)}, u32[]{:S(2)}) async-start(bf16[16,2,128,256]{3,2,1,0:T(8,128)(2,1)} %bitcast.55), calls=%async_computation.1 | async-start | bytes 4194304 | tf_op jit(solution)/shard_map/all_to_all | solution.py:287
  45.1 0.1 copy.33
  45.1 0.1 copy.32
  45.2 0.1 reshape.134
  45.3 0.1 reshape.150
  45.4 2.8 %pad_maximum_fusion = bf16[40,128,256]{2,1,0:T(8,128)(2,1)} fusion(bf16[32,128,256]{2,1,0:T(8,128)(2,1)S(1)} %bitcast.119, bf16[8,128,256]{2,1,0:T(8,128)(2,1)} %bitcast.124), kind=kLoop, calls=%fused_computation.7 | loop fusion | flops 1310720 | bytes 5242880 | tf_op jit(solution)/shard_map/concatenate | solution.py:273
  48.2 2.4 %gather_fusion = bf16[32,128,256]{2,1,0:T(8,128)(2,1)S(1)} fusion(bf16[40,128,256]{2,1,0:T(8,128)(2,1)} %pad_maximum_fusion, s32[1024]{0:T(1024)S(1)} %pad_clamp_fusion), kind=kCustom, calls=%fused_computation | custom fusion | bytes 4194432 | tf_op jit(solution)/shard_map/gather | solution.py:210
  50.6 0.5 fusion.2
  51.2 0.8 copy-done.4
  52.0 0.3 fusion.17
  52.3 1.4 multiply_convert_fusion.2
  53.6 16.6 %all-to-all-done.1 = bf16[16,2,128,256]{3,2,1,0:T(8,128)(2,1)} async-done(((bf16[16,2,128,256]{3,2,1,0:T(8,128)(2,1)}), bf16[16,2,128,256]{3,2,1,0:T(8,128)(2,1)}, u32[]{:S(2)}, u32[]{:S(2)}) %all-to-all-start.1) | async-done | bytes 2097184 | tf_op jit(solution)/shard_map/all_to_all | solution.py:287
  70.2 3.3 %pad_maximum_fusion.1 = bf16[40,128,256]{2,1,0:T(8,128)(2,1)} fusion(bf16[32,128,256]{2,1,0:T(8,128)(2,1)} %bitcast.13, bf16[8,128,256]{2,1,0:T(8,128)(2,1)S(1)} %bitcast.132), kind=kLoop, calls=%fused_computation.8 | loop fusion | flops 1310720 | bytes 5242880 | tf_op jit(solution)/shard_map/concatenate | solution.py:273
  73.5 2.4 %gather_fusion.1 = bf16[32,128,256]{2,1,0:T(8,128)(2,1)S(1)} fusion(bf16[40,128,256]{2,1,0:T(8,128)(2,1)} %pad_maximum_fusion.1, s32[1024]{0:T(1024)S(1)} %pad_clamp_fusion), kind=kCustom, calls=%fused_computation.1 | custom fusion | bytes 4194432 | tf_op jit(solution)/shard_map/gather | solution.py:210
  76.0 0.5 fusion.3
  76.5 0.3 copy-done.14
  76.9 0.3 fusion.18
  77.2 0.4 multiply_convert_fusion.1
  77.7 0.2 copy-done.20
  77.9 0.3 select_reduce_fusion
  78.2 0.2 convolution_multiply_fusion.5
  78.4 0.5 fusion.1
  79.0 0.8 copy-done.11
  79.8 0.3 convolution_convert_fusion.3
  80.1 2.7 %fusion.5 = f32[8,256,4,128]{3,1,2,0:T(8,128)} fusion(bf16[8,128,256,1]{2,1,3,0:T(8,128)(2,1)S(1)} %bitcast.129, bf16[1,1,8,4,128,128]{5,4,3,2,1,0:T(8,128)(2,1)S(1)} %copy-done), kind=kOutput, calls=%fused_computation.26 | convolution fusion | flops 268435456 | bytes 5767168 | tf_op jit(solution)/shard_map/bkij,bid->bkjd/dot_general | solution.py:215
  82.8 5.7 %copy.35 = f32[32,128,256]{2,1,0:T(8,128)} copy(f32[32,128,256]{1,2,0:T(8,128)} %bitcast.116) | data formatting | bytes 8388608 | tf_op jit(solution)/shard_map/reshape | solution.py:218
  88.5 2.9 %broadcast_in_dim.25 = f32[40,128,256]{2,1,0:T(8,128)} broadcast(f32[]{:T(128)} %constant.8.clone.1), dimensions={} | broadcast | bytes 5242884 | tf_op jit(solution)/shard_map/broadcast_in_dim | solution.py:219
  91.4 10.1 %scatter_fusion = f32[40,128,256]{2,1,0:T(8,128)} fusion(f32[40,128,256]{2,1,0:T(8,128)} %broadcast_in_dim.25, s32[32]{0:T(128)S(1)} %reshape.150, f32[32,128,256]{2,1,0:T(8,128)} %copy.35), kind=kCustom, calls=%fused_computation.2 | custom fusion | flops 1048576 | bytes 12583040 | tf_op jit(solution)/shard_map/scatter-add | solution.py:219
  101.5 1.3 slice.31
  102.8 3.8 %slice.35 = bf16[32,128,256]{2,1,0:T(8,128)(2,1)} slice(f32[40,128,256]{2,1,0:T(8,128)} %scatter_fusion), slice={[8:40], [0:128], [0:256]} | slice | bytes 4194304 | tf_op jit(solution)/shard_map/slice | solution.py:321
  106.7 0.1 copy.38
  106.8 0.1 reshape.162
  106.9 7.2 %all-to-all-start.2 = ((bf16[16,2,128,256]{3,2,1,0:T(8,128)(2,1)}), bf16[16,2,128,256]{3,2,1,0:T(8,128)(2,1)}, u32[]{:S(2)}, u32[]{:S(2)}) async-start(bf16[16,2,128,256]{3,2,1,0:T(8,128)(2,1)} %bitcast.27), calls=%async_computation.2 | async-start | bytes 4194304 | tf_op jit(solution)/shard_map/all_to_all | solution.py:325
  114.2 2.8 %multiply_convert_fusion = (bf16[1024,256]{1,0:T(8,128)(2,1)S(1)}, bf16[1,1,1024,256]{3,2,1,0:T(8,128)(2,1)}) fusion(f32[1024,256]{1,0:T(8,128)} %get-tuple-element.36, bf16[1,1,1024,256]{3,2,1,0:T(8,128)(2,1)} %param.15, f32[1024,256]{1,0:T(8,128)S(1)} %bitcast.130, bf16[1024,256]{1,0:T(8,128)(2,1)S(1)} %copy-done.12, bf16[256,256]{1,0:T(8,128)(2,1)S(1)} %copy-done.19), kind=kOutput, calls=%fused_computation.30 | convolution fusion | flops 137625600 | bytes 4325376 | tf_op jit(solution)/shard_map/dot_general | solution.py:229
  117.0 0.8 copy-done.22
  117.8 1.0 fusion.4
  118.8 1.1 copy.37
  119.9 0.6 subtract_reduce_fusion
  121.2 1.4 convolution_multiply_fusion.2
  122.7 0.3 convolution_multiply_fusion.1
  123.0 0.3 convolution_multiply_fusion.4
  123.4 0.1 pad_maximum_fusion.2
  123.5 0.7 broadcast_in_dim.29
  124.2 1.3 concatenate.13.x_ref
  125.5 59.0 %shard_map.196 = f32[2,16,40,256]{3,2,1,0:T(8,128)S(1)} custom-call(f32[2,16,40,256]{3,2,1,0:T(8,128)S(1)} %concatenate.13.x_ref), custom_call_target="tpu_custom_call" | custom-call | tf_op jit(solution)/shard_map/pallas_call | solution.py:182
  184.6 0.6 slice.26
  185.1 0.5 copy-done.1
  185.7 0.1 slice_reduce_fusion
  185.7 0.1 reshape_squeeze.15
  185.8 0.7 copy.40
  186.5 2.2 %fusion.16 = (f32[1,16,16,256]{3,2,1,0:T(8,128)}, f32[1,16,16,256]{3,2,1,0:T(8,128)}, f32[1,16,16,256]{3,2,1,0:T(8,128)}, f32[1,16,16,256]{3,2,1,0:T(8,128)}) fusion(f32[2,16,40,256]{3,2,1,0:T(8,128)} %copy-done.1), kind=kLoop, calls=%fused_computation.55 | loop fusion | bytes 2097152 | tf_op jit(solution)/shard_map/unstack | solution.py:353
  188.7 2.8 %copy.49 = bf16[4,8,128,256]{3,1,2,0:T(8,128)(2,1)S(1)} copy(bf16[4,8,128,256]{3,2,1,0:T(8,128)(2,1)} %bitcast.57) | data formatting | bytes 4194304
  191.5 0.5 convolution_convert_fusion.2
  192.0 1.0 broadcast_in_dim_reshape.3
  (47 shorter events, 0.2 us)
Async XLA Ops:
  0.6 50.0 %copy-start = (bf16[1,1,8,4,128,128]{5,4,3,2,1,0:T(8,128)(2,1)S(1)}, bf16[1,1,8,4,128,128]{5,4,3,2,1,0:T(8,128)(2,1)}, u32[]{:S(2)}) copy-start(bf16[1,1,8,4,128,128]{5,4,3,2,1,0:T(8,128)(2,1)} %param.16) | copy-start | bytes 3145732
  5.5 32.9 %all-to-all-start = ((bf16[16,2,128,256]{3,2,1,0:T(8,128)(2,1)}), bf16[16,2,128,256]{3,2,1,0:T(8,128)(2,1)S(1)}, u32[]{:S(2)}, u32[]{:S(2)}) async-start(bf16[16,2,128,256]{3,2,1,0:T(8,128)(2,1)} %bitcast.120), calls=%async_computation | async-start | bytes 4194304 | tf_op jit(solution)/shard_map/all_to_all | solution.py:277
  38.4 6.7 %copy-start.16 = (s32[1,1,8,4]{2,3,1,0:T(4,128)S(1)}, s32[1,1,8,4]{2,3,1,0:T(4,128)}, u32[]{:S(2)}) copy-start(s32[1,1,8,4]{2,3,1,0:T(4,128)} %param.17) | copy-start | bytes 388
  38.4 6.9 %copy-start.17 = (s32[1,1,1024]{2,1,0:T(1,128)S(1)}, s32[1,1,1024]{2,1,0:T(1,128)}, u32[]{:S(2)}) copy-start(s32[1,1,1024]{2,1,0:T(1,128)} %param.20) | copy-start | bytes 12292
  38.4 31.8 %all-to-all-start.1 = ((bf16[16,2,128,256]{3,2,1,0:T(8,128)(2,1)}), bf16[16,2,128,256]{3,2,1,0:T(8,128)(2,1)}, u32[]{:S(2)}, u32[]{:S(2)}) async-start(bf16[16,2,128,256]{3,2,1,0:T(8,128)(2,1)} %bitcast.55), calls=%async_computation.1 | async-start | bytes 4194304 | tf_op jit(solution)/shard_map/all_to_all | solution.py:287
  50.6 1.4 copy-start.15
  50.6 1.6 copy-start.2
  50.6 1.6 copy-start.18
  51.2 0.8 copy-start.4
  53.6 16.6 %copy-start.8 = (bf16[1024,256]{1,0:T(8,128)(2,1)}, bf16[1024,256]{1,0:T(8,128)(2,1)S(1)}, u32[]{:S(2)}) copy-start(bf16[1024,256]{1,0:T(8,128)(2,1)S(1)} %get-tuple-element.35) | copy-start | bytes 1572868
  76.0 0.9 copy-start.14
  76.0 1.2 copy-start.9
  76.0 1.2 copy-start.19
  76.5 1.1 copy-start.6
  77.2 0.7 copy-start.20
  77.2 0.7 copy-start.21
  79.0 0.8 copy-start.11
  106.9 7.3 %copy-start.12 = (bf16[1024,256]{1,0:T(8,128)(2,1)S(1)}, bf16[1024,256]{1,0:T(8,128)(2,1)}, u32[]{:S(2)}) copy-start(bf16[1024,256]{1,0:T(8,128)(2,1)} %copy-done.11) | copy-start | bytes 1572868
  106.9 81.8 %all-to-all-start.2 = ((bf16[16,2,128,256]{3,2,1,0:T(8,128)(2,1)}), bf16[16,2,128,256]{3,2,1,0:T(8,128)(2,1)}, u32[]{:S(2)}, u32[]{:S(2)}) async-start(bf16[16,2,128,256]{3,2,1,0:T(8,128)(2,1)} %bitcast.27), calls=%async_computation.2 | async-start | bytes 4194304 | tf_op jit(solution)/shard_map/all_to_all | solution.py:325
  114.2 3.6 %copy-start.3 = (bf16[1,1,1024,256]{3,2,1,0:T(8,128)(2,1)S(1)}, bf16[1,1,1024,256]{3,2,1,0:T(8,128)(2,1)}, u32[]{:S(2)}) copy-start(bf16[1,1,1024,256]{3,2,1,0:T(8,128)(2,1)} %param.13) | copy-start | bytes 1572868
  114.2 7.0 %copy-start.7 = (bf16[8,256,128]{1,2,0:T(8,128)(2,1)S(1)}, bf16[8,256,128]{1,2,0:T(8,128)(2,1)}, u32[]{:S(2)}) copy-start(bf16[8,256,128]{1,2,0:T(8,128)(2,1)} %copy-done.6) | copy-start | bytes 1572868
  117.0 0.8 copy-start.22
  117.0 5.6 %copy-start.10 = (bf16[1024,256]{1,0:T(8,128)(2,1)S(1)}, bf16[1024,256]{1,0:T(8,128)(2,1)}, u32[]{:S(2)}) copy-start(bf16[1024,256]{1,0:T(8,128)(2,1)} %copy-done.8) | copy-start | bytes 1572868
  117.0 5.6 %copy-start.13 = (bf16[1024,256]{1,0:T(8,128)(2,1)S(1)}, bf16[1024,256]{1,0:T(8,128)(2,1)}, u32[]{:S(2)}) copy-start(bf16[1024,256]{1,0:T(8,128)(2,1)} %copy-done.11) | copy-start | bytes 1572868
  117.8 5.2 %copy-start.5 = (bf16[8,256,128]{1,2,0:T(8,128)(2,1)S(1)}, bf16[8,256,128]{1,2,0:T(8,128)(2,1)}, u32[]{:S(2)}) copy-start(bf16[8,256,128]{1,2,0:T(8,128)(2,1)} %copy-done.4) | copy-start | bytes 1572868
  121.2 1.8 copy-start.23
  184.6 1.1 copy-start.1

commit v2 on v1

v2 whole, which is shorter than its diff:
```python
import functools

import jax
import jax.numpy as jnp
from jax import lax
from jax.experimental import pallas as pl
from jax.experimental.pallas import tpu as pltpu
from jax.sharding import PartitionSpec as P

MESH = pl.DeviceIdType.MESH
F32 = jnp.float32
BF16 = jnp.bfloat16
NB = 8
K = 4
S = 2
BLK = 128
D = 256
TB = 32
TILES = NB * K
CHUNK = 2
ROWS = CHUNK * BLK
CHUNKS = NB // CHUNK
LANES = 128


def nn(a, b):
    return jnp.dot(a, b, preferred_element_type=F32)


def nt(a, b):
    return lax.dot_general(a, b, (((1,), (1,)), ((), ())), preferred_element_type=F32)


def tn(a, b):
    return lax.dot_general(a, b, (((0,), (0,)), ((), ())), preferred_element_type=F32)


def sigmoid(v):
    return 0.5 * jnp.tanh(0.5 * v) + 0.5


def slope(v):
    q = sigmoid(v)
    return q * (1.0 + v * (1.0 - q))


def program_kernel(
    groups, depth,
    tab, feat_in, hist_in, aux_in, tiles_in, bins, flags, w_nf, w_sf, w_ns, w_ss, w_hz,
    o_hist, o_hidden, o_aux, o_nf, o_sf, o_ns, o_ss, o_hz, o_loss,
    own, past, aux, tiles, turned, table1, table2, stage1, stage2, agg1, agg2, pre1, hid2, gp2,
    gp1, glog, chain, came, fold, loss_acc,
    pack, total, acc, from_core, from_grp, mine, from_z, done,
    load_sem, f_send, f_recv, h_send, h_recv, b_send, b_recv,
    core_sem, g_send, g_recv, z_send, z_recv, zb_send, zb_recv, r_send, r_recv, w_send, w_recv,
):
    slots = groups * S
    t_src = 0
    t_snd = t_src + TILES
    t_prev = t_snd + slots
    t_last = t_prev + TILES
    t_qprev = t_last + NB + slots
    t_qlast = t_qprev + slots
    rows_of = D // groups
    piece = 2 * rows_of + 8
    units = piece // 4
    scale = 1.0 / (NB * BLK * groups)

    clus = lax.axis_index("clus")
    g = lax.axis_index("grp")
    core = lax.rem(clus, 2)
    z = clus // 2
    sibling = clus + 1 - 2 * core

    def grp_peer(d):
        return lax.rem(g + d, groups)

    def z_peer(d):
        return lax.rem(z + d, depth)

    loads = [
        pltpu.make_async_copy(feat_in, own, load_sem.at[0]),
        pltpu.make_async_copy(hist_in, past, load_sem.at[1]),
        pltpu.make_async_copy(feat_in, table1.at[pl.ds(0, NB)], load_sem.at[2]),
        pltpu.make_async_copy(tiles_in, tiles, load_sem.at[3]),
        pltpu.make_async_copy(aux_in, aux, load_sem.at[4]),
    ]
    for load in loads:
        load.start()

    barrier = pltpu.get_barrier_semaphore()
    pl.semaphore_signal(barrier, inc=1, device_id={"clus": sibling}, device_id_type=MESH)

    @pl.loop(1, groups)
    def _(d):
        pl.semaphore_signal(barrier, inc=1, device_id={"grp": grp_peer(d)}, device_id_type=MESH)

    @pl.loop(1, depth)
    def _(d):
        pl.semaphore_signal(
            barrier, inc=1, device_id={"clus": z_peer(d) * 2 + core}, device_id_type=MESH
        )

    blank = jnp.zeros((S, BLK, D), BF16)
    table1[pl.ds(NB + g * S, S)] = blank
    table2[pl.ds(NB + g * S, S)] = blank
    came[pl.ds(g * S, S)] = blank
    chain[TILES] = jnp.zeros((BLK, D), F32)
    fold[slots] = jnp.zeros((BLK, D), F32)
    pack[:, :, 2 * rows_of :, :] = jnp.zeros((2, groups, 8, D), F32)

    pl.semaphore_wait(barrier, groups + depth - 1)

    def exchange(stage, target, base, send, recv):
        def out(d):
            p = grp_peer(d)
            return pltpu.make_async_remote_copy(
                src_ref=stage.at[pl.ds(p * S, S)], dst_ref=target.at[pl.ds(base + g * S, S)],
                send_sem=send.at[p], recv_sem=recv.at[g],
                device_id={"grp": p}, device_id_type=MESH,
            )

        def into(d):
            p = grp_peer(d)
            return pltpu.make_async_remote_copy(
                src_ref=stage.at[pl.ds(p * S, S)], dst_ref=target.at[pl.ds(base + p * S, S)],
                send_sem=send.at[p], recv_sem=recv.at[p],
                device_id={"grp": p}, device_id_type=MESH,
            )

        return out, into

    f_out, f_in = exchange(stage1, table1, NB, f_send, f_recv)
    h_out, h_in = exchange(stage2, table2, NB, h_send, h_recv)
    b_out, b_in = exchange(stage1, came, 0, b_send, b_recv)

    loads[0].wait()

    @pl.loop(1, groups)
    def _(d):
        p = grp_peer(d)
        for s in range(S):
            stage1[p * S + s] = own[tab[t_snd + p * S + s]]
        f_out(d).start()

    loads[1].wait()

    @pl.loop(1, groups)
    def _(d):
        p = grp_peer(d)
        for s in range(S):
            stage2[p * S + s] = past[tab[t_snd + p * S + s]]
        f_out(d).wait_send()
        h_out(d).start()

    loads[3].wait()

    @pl.loop(0, NB)
    def _(b):
        for k in range(K):
            turned[b, pl.ds(k * BLK, BLK), :] = tiles[b, k].T

    loads[2].wait()

    @pl.loop(1, groups)
    def _(d):
        f_in(d).wait_recv()

    def aggregate(table, b):
        wide = jnp.concatenate([tiles[b, k] for k in range(K)], axis=1)
        deep = jnp.concatenate([table[tab[t_src + b * K + k]] for k in range(K)], axis=0)
        return nn(wide, deep).astype(BF16)

    @pl.loop(0, CHUNKS)
    def _(c):
        a = jnp.concatenate([aggregate(table1, c * CHUNK + j) for j in range(CHUNK)], axis=0)
        rows = pl.ds(pl.multiple_of(c * ROWS, ROWS), ROWS)
        blocks = pl.ds(c * CHUNK, CHUNK)
        agg1[rows, :] = a
        pre = nn(a, w_nf[...]) + nn(own[blocks].reshape(ROWS, D), w_sf[...])
        pre1[rows, :] = pre
        h = (pre * sigmoid(pre)).astype(BF16)
        table2[blocks] = h.reshape(CHUNK, BLK, D)
        o_hist[rows, :] = h

    loss_acc[...] = jnp.zeros((TB, ROWS), F32)

    @pl.loop(1, groups)
    def _(d):
        h_in(d).wait_recv()

    @pl.loop(0, CHUNKS)
    def _(c):
        a = jnp.concatenate([aggregate(table2, c * CHUNK + j) for j in range(CHUNK)], axis=0)
        rows = pl.ds(pl.multiple_of(c * ROWS, ROWS), ROWS)
        blocks = pl.ds(c * CHUNK, CHUNK)
        agg2[rows, :] = a
        pre = nn(a, w_ns[...]) + nn(table2[blocks].reshape(ROWS, D), w_ss[...])
        q = sigmoid(pre)
        h = (pre * q).astype(BF16)
        hid2[rows, :] = h
        logits = nt(w_hz[...], h)
        step = lax.broadcasted_iota(jnp.int32, (TB, ROWS), 0)
        bin_row = bins[c]
        flag_row = flags[c].astype(F32)
        counted = step <= bin_row
        event = jnp.where(step == bin_row, flag_row, 0.0)
        soft = jnp.maximum(logits, 0.0) + jnp.log1p(jnp.exp(-jnp.abs(logits)))
        loss_acc[...] += jnp.where(counted, soft, 0.0) - event * logits
        gl = (jnp.where(counted, sigmoid(logits), 0.0) - event).astype(BF16)
        glog[:, rows] = gl
        gp = (tn(gl, w_hz[...]) * (q * (1.0 + pre * (1.0 - q)))).astype(BF16)
        gp2[rows, :] = gp
        ga = nt(gp, w_ns[...]).astype(BF16)
        for j in range(CHUNK):
            b = c * CHUNK + j
            spread = nn(turned[b], ga[j * BLK : (j + 1) * BLK])
            for k in range(K):
                i = b * K + k
                chain[i] = spread[k * BLK : (k + 1) * BLK] + chain[tab[t_prev + i]]

    @pl.loop(1, groups)
    def _(d):
        p = grp_peer(d)
        for s in range(S):
            stage1[p * S + s] = chain[tab[t_last + NB + p * S + s]].astype(BF16)
        b_out(d).start()

    loads[4].wait()

    def put(half, base, value):
        pack[half, :, pl.ds(base, rows_of), :] = (value * scale).reshape(groups, rows_of, D)

    put(0, rows_of, tn(agg2[...], gp2[...]))
    put(1, rows_of, tn(table2[pl.ds(0, NB)].reshape(NB * BLK, D), gp2[...]))
    hz = nn(glog[...], hid2[...]) * scale
    for t in range(TB // 8):
        pack[t // 2, t % 2, pl.ds(2 * rows_of, 8), :] = hz[t * 8 : (t + 1) * 8]
    loss = jnp.sum(loss_acc[...], keepdims=True) * scale
    pack[0, 2, pl.ds(2 * rows_of, 8), :] = jnp.broadcast_to(loss, (8, D))

    @pl.loop(0, CHUNKS)
    def _(c):
        rows = pl.ds(pl.multiple_of(c * ROWS, ROWS), ROWS)
        local = jnp.concatenate(
            [chain[tab[t_last + c * CHUNK + j]] for j in range(CHUNK)], axis=0
        )
        grad = local + nt(gp2[rows, :], w_ss[...]) + aux[rows, :].astype(F32)
        o_hidden[rows, :] = grad.astype(BF16)
        gp1[rows, :] = (grad * slope(pre1[rows, :])).astype(BF16)

    put(0, 0, tn(agg1[...], gp1[...]))
    put(1, 0, tn(own[...].reshape(NB * BLK, D), gp1[...]))

    swap = pltpu.make_async_remote_copy(
        src_ref=pack.at[1 - core], dst_ref=from_core, send_sem=core_sem.at[0],
        recv_sem=core_sem.at[1], device_id={"clus": sibling}, device_id_type=MESH,
    )
    swap.start()
    swap.wait()
    acc[...] = pack[core] + from_core[...]

    def spread_out(d):
        p = grp_peer(d)
        return pltpu.make_async_remote_copy(
            src_ref=acc.at[p], dst_ref=from_grp.at[g], send_sem=g_send.at[p],
            recv_sem=g_recv.at[g], device_id={"grp": p}, device_id_type=MESH,
        )

    @pl.loop(1, groups)
    def _(d):
        spread_out(d).start()

    mine[...] = acc[g]

    @pl.loop(1, groups)
    def _(d):
        b_in(d).wait_recv()

    @pl.loop(0, slots)
    def _(i):
        fold[i] = came[i].astype(F32) + fold[tab[t_qprev + i]]

    @pl.loop(0, NB)
    def _(j):
        o_aux[j] = fold[tab[t_qlast + j]].astype(BF16)

    @pl.loop(1, groups)
    def _(d):
        p = grp_peer(d)
        pltpu.make_async_remote_copy(
            src_ref=acc.at[p], dst_ref=from_grp.at[p], send_sem=g_send.at[p],
            recv_sem=g_recv.at[p], device_id={"grp": p}, device_id_type=MESH,
        ).wait_recv()
        mine[...] += from_grp[p]

    def owner(u):
        return (u * depth) // units

    def lot(u):
        return u if depth < units else 0

    def unit_of(ref, u):
        return ref.at[pl.ds(8 * (u // 2), 8), pl.ds(LANES * (u % 2), LANES)]

    def to_owner(u):
        return pltpu.make_async_remote_copy(
            src_ref=unit_of(mine, u), dst_ref=from_z.at[lot(u), z], send_sem=z_send.at[u],
            recv_sem=z_recv.at[lot(u), z], device_id={"clus": owner(u) * 2 + core},
            device_id_type=MESH,
        )

    for u in range(units):
        @pl.when(z != owner(u))
        def _():
            to_owner(u).start()

    def share(u, d):
        q = z_peer(d)
        return pltpu.make_async_remote_copy(
            src_ref=unit_of(done, u), dst_ref=unit_of(done, u), send_sem=zb_send.at[lot(u), q],
            recv_sem=zb_recv.at[u], device_id={"clus": q * 2 + core}, device_id_type=MESH,
        )

    for u in range(units):
        @pl.when(z == owner(u))
        def _():
            def gather(d, partial):
                q = z_peer(d)
                pltpu.make_async_remote_copy(
                    src_ref=unit_of(mine, u), dst_ref=from_z.at[lot(u), q],
                    send_sem=z_send.at[u], recv_sem=z_recv.at[lot(u), q],
                    device_id={"clus": q * 2 + core}, device_id_type=MESH,
                ).wait_recv()
                return partial + from_z[lot(u), q]

            unit_of(done, u)[...] = lax.fori_loop(1, depth, gather, unit_of(mine, u)[...])

            @pl.loop(1, depth)
            def _(d):
                share(u, d).start()

    for u in range(units):
        @pl.when(z != owner(u))
        def _():
            to_owner(u).wait_send()
            share(u, 1).wait_recv()

    def publish(d, slot):
        p = grp_peer(d)
        return pltpu.make_async_remote_copy(
            src_ref=done, dst_ref=total.at[core, slot], send_sem=r_send.at[p],
            recv_sem=r_recv.at[slot], device_id={"grp": p}, device_id_type=MESH,
        )

    def forward(half, p):
        return pltpu.make_async_remote_copy(
            src_ref=total.at[half, p], dst_ref=total.at[half, p], send_sem=w_send.at[p],
            recv_sem=w_recv.at[p], device_id={"clus": sibling}, device_id_type=MESH,
        )

    @pl.loop(1, groups)
    def _(d):
        publish(d, g).start()

    total[core, g] = done[...]
    forward(core, g).start()

    @pl.loop(1, groups)
    def _(d):
        p = grp_peer(d)
        publish(d, p).wait_recv()
        forward(core, p).start()

    @pl.loop(0, groups)
    def _(p):
        forward(1 - core, p).wait_recv()

    def pick(half, base):
        return total[half, :, pl.ds(base, rows_of), :].reshape(D, D)

    o_nf[...] = pick(0, 0)
    o_sf[...] = pick(1, 0)
    o_ns[...] = pick(0, rows_of)
    o_ss[...] = pick(1, rows_of)
    for t in range(TB // 8):
        o_hz[pl.ds(t * 8, 8), :] = total[t // 2, t % 2, pl.ds(2 * rows_of, 8), :]
    o_loss[...] = total[0, 2, pl.ds(2 * rows_of, 8), pl.ds(0, LANES)]

    @pl.loop(1, groups)
    def _(d):
        h_out(d).wait_send()
        b_out(d).wait_send()
        spread_out(d).wait_send()
        publish(d, g).wait_send()

    @pl.loop(0, groups)
    def _(p):
        forward(core, p).wait_send()

    for u in range(units):
        @pl.when(z == owner(u))
        def _():
            @pl.loop(1, depth)
            def _(d):
                share(u, d).wait_send()


def latest(keys, queries, limits):
    count = keys.shape[0]
    place = jnp.arange(count, dtype=jnp.int32)[None, :]
    hit = (keys[None, :] == queries[:, None]) & (place < limits[:, None])
    found = jnp.max(jnp.where(hit, place, -1), axis=1)
    return jnp.where(found < 0, count, found)


def shards(
    features, history, aux_history, tile_values, tile_sources, send_list, event_bins, event_flags,
    neigh_first, self_first, neigh_second, self_second, hazard_weight,
):
    groups = lax.axis_size("grp")
    depth = lax.axis_size("clus") // 2
    slots = groups * S
    rows_of = D // groups
    piece = 2 * rows_of + 8
    units = piece // 4
    lots = units if depth < units else 1
    src = tile_sources.reshape(TILES)
    snd = send_list.reshape(slots)
    ints = lambda n: jnp.arange(n, dtype=jnp.int32)
    full = lambda n, v: jnp.full((n,), v, jnp.int32)
    tab = jnp.concatenate(
        [
            src,
            jnp.minimum(snd, NB - 1),
            latest(
                src,
                jnp.concatenate([src, ints(NB + slots)]),
                jnp.concatenate([ints(TILES), full(NB + slots, TILES)]),
            ),
            latest(
                snd,
                jnp.concatenate([snd, ints(NB)]),
                jnp.concatenate([ints(slots), full(NB, slots)]),
            ),
        ]
    )
    any_spec = pl.BlockSpec(memory_space=pl.ANY)
    vmem = pl.BlockSpec(memory_space=pltpu.VMEM)
    dma = pltpu.SemaphoreType.DMA
    nodes = NB * BLK
    out_shape = (
        jax.ShapeDtypeStruct((nodes, D), BF16),
        jax.ShapeDtypeStruct((nodes, D), BF16),
        jax.ShapeDtypeStruct((NB, BLK, D), BF16),
        jax.ShapeDtypeStruct((D, D), F32),
        jax.ShapeDtypeStruct((D, D), F32),
        jax.ShapeDtypeStruct((D, D), F32),
        jax.ShapeDtypeStruct((D, D), F32),
        jax.ShapeDtypeStruct((TB, D), F32),
        jax.ShapeDtypeStruct((8, LANES), F32),
    )
    scratch = [
        pltpu.VMEM((NB, BLK, D), BF16),
        pltpu.VMEM((NB, BLK, D), BF16),
        pltpu.VMEM((nodes, D), BF16),
        pltpu.VMEM((NB, K, BLK, BLK), BF16),
        pltpu.VMEM((NB, K * BLK, BLK), BF16),
        pltpu.VMEM((NB + slots, BLK, D), BF16),
        pltpu.VMEM((NB + slots, BLK, D), BF16),
        pltpu.VMEM((slots, BLK, D), BF16),
        pltpu.VMEM((slots, BLK, D), BF16),
        pltpu.VMEM((nodes, D), BF16),
        pltpu.VMEM((nodes, D), BF16),
        pltpu.VMEM((nodes, D), F32),
        pltpu.VMEM((nodes, D), BF16),
        pltpu.VMEM((nodes, D), BF16),
        pltpu.VMEM((nodes, D), BF16),
        pltpu.VMEM((TB, nodes), BF16),
        pltpu.VMEM((TILES + 1, BLK, D), F32),
        pltpu.VMEM((slots, BLK, D), BF16),
        pltpu.VMEM((slots + 1, BLK, D), F32),
        pltpu.VMEM((TB, ROWS), F32),
        pltpu.VMEM((2, groups, piece, D), F32),
        pltpu.VMEM((2, groups, piece, D), F32),
        pltpu.VMEM((groups, piece, D), F32),
        pltpu.VMEM((groups, piece, D), F32),
        pltpu.VMEM((groups, piece, D), F32),
        pltpu.VMEM((piece, D), F32),
        pltpu.VMEM((lots, depth, 8, LANES), F32),
        pltpu.VMEM((piece, D), F32),
        dma((5,)),
        dma((groups,)), dma((groups,)), dma((groups,)), dma((groups,)), dma((groups,)),
        dma((groups,)),
        dma((2,)), dma((groups,)), dma((groups,)), dma((units,)), dma((lots, depth)),
        dma((lots, depth)), dma((units,)), dma((groups,)), dma((groups,)), dma((groups,)),
        dma((groups,)),
    ]
    outs = pl.pallas_call(
        functools.partial(program_kernel, groups, depth),
        out_shape=out_shape,
        in_specs=[pl.BlockSpec(memory_space=pltpu.SMEM)] + [any_spec] * 4 + [vmem] * 7,
        out_specs=(vmem,) * 9,
        scratch_shapes=scratch,
        compiler_params=pltpu.CompilerParams(
            collective_id=0, has_side_effects=True, vmem_limit_bytes=56 << 20
        ),
    )(
        tab,
        features.reshape(NB, BLK, D),
        history.reshape(NB, BLK, D),
        aux_history.reshape(nodes, D),
        tile_values.reshape(NB, K, BLK, BLK),
        event_bins.reshape(CHUNKS, 1, ROWS),
        event_flags.reshape(CHUNKS, 1, ROWS),
        neigh_first, self_first, neigh_second, self_second, hazard_weight.T,
    )
    hist, hidden, aux, nf, sf, ns, ss, hz, loss = outs
    return (
        hist[None, None], hidden[None, None], aux.reshape(1, 1, nodes, D),
        nf, sf, ns, ss, hz.T, loss[0, 0],
    )


def solution(mesh):
    in_specs = (
        P("clus", "grp", None, None),
        P("clus", "grp", None, None),
        P("clus", "grp", None, None),
        P("clus", "grp", None, None, None, None),
        P("clus", "grp", None, None),
        P("clus", "grp", None, None),
        P("clus", "grp", None),
        P("clus", "grp", None),
        P(), P(), P(), P(), P(),
    )
    out_specs = (
        P("clus", "grp", None, None),
        P("clus", "grp", None, None),
        P("clus", "grp", None, None),
        P(), P(), P(), P(), P(), P(),
    )
    return jax.shard_map(shards, mesh=mesh, in_specs=in_specs, out_specs=out_specs, check_vma=False)
```

time: 194 us -> 168 us (0.87)
  Pallas kernels: 59 us -> 153 us
  waiting for transfers between devices: 36.2 us -> 0 us
  local copies, waits for them, and re-layouts: 41.2 us -> 12.8 us
  starting transfers between devices: 21.5 us -> 0 us
  matrix products: 16.5 us -> 0 us
  other arithmetic: 16.8 us -> 0.98 us
    pallas_call x1, Pallas kernels: 59 us -> 153 us  [shards(): pl.pallas_call(functools.partial(program_kernel, groups, depth), out_shap...]
    all_to_all x3 -> x0, waiting for transfers between devices: 36.2 us -> none  [the longest x1 19.6 us: shards(): lax.all_to_all(outgoing(own_rows), 'grp', split_axis=0, concat_axis=0, ti...]
    all_to_all x3 -> x0, starting transfers between devices: 21.5 us -> none  [the longest x1 7.58 us: shards(): lax.all_to_all(outgoing(own_rows), 'grp', split_axis=0, concat_axis=0, ti...]
    dot_general x19 -> x0, matrix products: 16.5 us -> none  [the longest x6 3.87 us: transpose_dot(): lax.dot_general(former, latter, (((0,), (0,)), ((), ())), preferred_eleme...]
    scatter-add x1 -> x0, other arithmetic: 10.1 us -> none  [spread_back(): jax.ops.segment_sum(flattened, sources.reshape(-1), num_segments=table_size)]
    another operation x6 -> x0, local copies, waits for them, and re-layouts: 6.74 us -> none  [the longest x2 3.37 us: outgoing(): flattened = values.reshape(block_count, block_rows * feat_width)]
    reshape x2, local copies, waits for them, and re-layouts: 5.8 us -> 0.17 us  [the longest x1 0.09 us: shards(): snd = send_list.reshape(slots)]
    concatenate x2 -> x3, other arithmetic: 6.08 us -> 0.79 us  [the longest x1 0.64 us: shards(): jnp.concatenate([src, jnp.minimum(snd, NB - 1), latest(src, jnp.concatena...]
  transfers between devices with their start and end apart: 3 -> 0, of which waited for: 2 -> 0; matrix products, arithmetic and copies ran while one was open for 14% -> 0% of each run, Pallas kernels for 31% -> 0%
where the time goes in v2:
time: 168 us; the launch traced here: 167 us
  Pallas kernels  153 us (91%)
  local copies, waits for them, and re-layouts  12.8 us (8%)
    pallas_call x1, Pallas kernels, shards(): pl.pallas_call(functools.partial(program_kernel, groups, depth), out_shap...  153 us
    unnamed x32, local copies, waits for them, and re-layouts  11.4 us

profile of v2, /device:TPU:1, one launch (start us, length us, event | category | flops | bytes accessed | tf_op | source)
XLA Modules:
  0.0 167.2 jit_solution(10635491464314324731)
XLA Ops:
  0.6 0.0 copy-start.7
  0.7 0.7 copy-done.7
  1.3 0.1 copy.26
  1.4 0.1 reshape.51
  1.5 0.0 copy-start.9
  1.5 0.1 pad_add_fusion.1
  1.6 0.6 copy-done.9
  2.1 0.1 select_reduce_fusion.1
  2.2 0.0 copy-start.8
  2.3 0.7 copy-done.8
  2.9 0.1 copy.27
  3.0 0.1 reshape.52
  3.1 0.0 copy-start.10
  3.1 0.1 pad_add_fusion.2
  3.2 0.6 copy-done.10
  3.7 0.1 select_reduce_fusion
  3.9 0.6 pad_add_fusion.tab
  4.5 152.7 %shard_map.196 = (bf16[1024,256]{1,0:T(8,128)(2,1)}, bf16[1024,256]{1,0:T(8,128)(2,1)}, bf16[8,128,256]{2,1,0:T(8,128)(2,1)}, f32[256,256]{1,0:T(8,128)}, f32[25...) custom-call(s32[176]{0:T(256)} %pad_add_fusion.tab, ...), custom_call_target="tpu_custom_call" | custom-call | tf_op jit(solution)/shard_map/pallas_call | solution.py:499
  157.2 1.2 slice.3
  158.4 0.0 copy-start.1
  158.4 1.9 %copy.36 = bf16[1,1,1024,256]{3,2,1,0:T(8,128)(2,1)} copy(bf16[1,1,1024,256]{3,2,1,0:T(8,128)(2,1)} %bitcast.19) | data formatting | bytes 1048576
  160.3 0.0 copy-done.1
  160.3 0.0 copy-start
  160.3 0.8 copy.37
  161.1 0.4 copy-done
  161.6 0.0 copy-start.5
  161.6 0.8 copy.38
  162.4 0.3 copy-done.5
  162.7 0.0 copy-start.4
  162.7 0.7 copy.39
  163.4 0.3 copy-done.4
  163.7 0.0 copy-start.3
  163.7 0.7 copy.40
  164.4 0.3 copy-done.3
  164.7 0.0 copy-start.2
  164.8 0.7 copy.41
  165.5 0.3 copy-done.2
  165.8 0.0 copy-start.6
  165.8 0.7 copy.42
  166.5 0.1 copy-done.6
  166.6 0.6 copy.43
  (5 shorter events, 0.0 us)
Async XLA Ops:
  0.6 0.7 copy-start.7
  1.5 0.7 copy-start.9
  2.2 0.7 copy-start.8
  3.1 0.7 copy-start.10
  158.4 1.9 %copy-start.1 = (bf16[1024,256]{1,0:T(8,128)(2,1)S(1)}, bf16[1024,256]{1,0:T(8,128)(2,1)}, u32[]{:S(2)}) copy-start(bf16[1024,256]{1,0:T(8,128)(2,1)} %get-tuple-element.19) | copy-start | bytes 1572868
  160.3 1.2 copy-start
  161.6 1.1 copy-start.5
  162.7 1.0 copy-start.4
  163.7 1.0 copy-start.3
  164.7 1.0 copy-start.2
  165.8 0.8 copy-start.6

commit v3 on v2

--- a/solution.py
+++ b/solution.py
@@ -21,6 +21,12 @@
 ROWS = CHUNK * BLK
 CHUNKS = NB // CHUNK
 LANES = 128
+PARTS = 4
+PART = S * BLK // PARTS
+ORDER = (
+    (2, 2), (1, 0), (0, 1), (3, 0), (0, 3), (1, 1), (3, 3), (1, 3),
+    (3, 1), (2, 0), (0, 2), (2, 1), (1, 2), (2, 3), (3, 2),
+)
 
 
 def nn(a, b):
@@ -46,11 +52,12 @@
 
 def program_kernel(
     groups, depth,
-    tab, feat_in, hist_in, aux_in, tiles_in, bins, flags, w_nf, w_sf, w_ns, w_ss, w_hz,
-    o_hist, o_hidden, o_aux, o_nf, o_sf, o_ns, o_ss, o_hz, o_loss,
+    tab, feat_in, hist_in, aux_in, tiles_in, bins_in, flags_in, nf_in, sf_in, ns_in, ss_in, hz_in,
+    x_hist, x_hidden, x_aux, x_total,
+    o_hist, o_hidden, o_aux, bins, flags, w_nf, w_sf, w_ns, w_ss, w_hz,
     own, past, aux, tiles, turned, table1, table2, stage1, stage2, agg1, agg2, pre1, hid2, gp2,
     gp1, glog, chain, came, fold, loss_acc,
-    pack, total, acc, from_core, from_grp, mine, from_z, done,
+    pack, total, acc, narrow, from_core, from_grp, mine, from_z, done, final,
     load_sem, f_send, f_recv, h_send, h_recv, b_send, b_recv,
     core_sem, g_send, g_recv, z_send, z_recv, zb_send, zb_recv, r_send, r_recv, w_send, w_recv,
 ):
@@ -78,12 +85,27 @@
     def z_peer(d):
         return lax.rem(z + d, depth)
 
+    side = int(groups ** 0.5)
+    gx = g // side
+    gy = lax.rem(g, side)
+    peers = [
+        lax.rem(gx + dx, side) * side + lax.rem(gy + dy, side)
+        for dx, dy in ORDER if dx < side and dy < side
+    ]
+
     loads = [
         pltpu.make_async_copy(feat_in, own, load_sem.at[0]),
         pltpu.make_async_copy(hist_in, past, load_sem.at[1]),
         pltpu.make_async_copy(feat_in, table1.at[pl.ds(0, NB)], load_sem.at[2]),
         pltpu.make_async_copy(tiles_in, tiles, load_sem.at[3]),
         pltpu.make_async_copy(aux_in, aux, load_sem.at[4]),
+        pltpu.make_async_copy(nf_in, w_nf, load_sem.at[5]),
+        pltpu.make_async_copy(sf_in, w_sf, load_sem.at[6]),
+        pltpu.make_async_copy(ns_in, w_ns, load_sem.at[7]),
+        pltpu.make_async_copy(ss_in, w_ss, load_sem.at[8]),
+        pltpu.make_async_copy(hz_in, w_hz, load_sem.at[9]),
+        pltpu.make_async_copy(bins_in, bins, load_sem.at[10]),
+        pltpu.make_async_copy(flags_in, flags, load_sem.at[11]),
     ]
     for load in loads:
         load.start()
@@ -112,46 +134,41 @@
     pl.semaphore_wait(barrier, groups + depth - 1)
 
     def exchange(stage, target, base, send, recv):
-        def out(d):
-            p = grp_peer(d)
+        def out(p, part):
+            s = part * PART // BLK
+            rows = pl.ds(pl.multiple_of(lax.rem(part * PART, BLK), PART), PART)
             return pltpu.make_async_remote_copy(
-                src_ref=stage.at[pl.ds(p * S, S)], dst_ref=target.at[pl.ds(base + g * S, S)],
+                src_ref=stage.at[p * S + s, rows], dst_ref=target.at[base + g * S + s, rows],
                 send_sem=send.at[p], recv_sem=recv.at[g],
                 device_id={"grp": p}, device_id_type=MESH,
             )
 
-        def into(d):
-            p = grp_peer(d)
+        def whole(p):
             return pltpu.make_async_remote_copy(
                 src_ref=stage.at[pl.ds(p * S, S)], dst_ref=target.at[pl.ds(base + p * S, S)],
                 send_sem=send.at[p], recv_sem=recv.at[p],
                 device_id={"grp": p}, device_id_type=MESH,
             )
 
-        return out, into
-
-    f_out, f_in = exchange(stage1, table1, NB, f_send, f_recv)
-    h_out, h_in = exchange(stage2, table2, NB, h_send, h_recv)
-    b_out, b_in = exchange(stage1, came, 0, b_send, b_recv)
+        def post(load, first, last):
+            @pl.loop(first, last)
+            def _(part):
+                s = part * PART // BLK
+                rows = pl.ds(pl.multiple_of(lax.rem(part * PART, BLK), PART), PART)
+                for p in peers:
+                    stage[p * S + s, rows] = load(p * S + s, rows).astype(BF16)
+                    out(p, part).start()
+
+        return post, whole
+
+    f_post, f_whole = exchange(stage1, table1, NB, f_send, f_recv)
+    h_post, h_whole = exchange(stage2, table2, NB, h_send, h_recv)
+    b_post, b_whole = exchange(stage1, came, 0, b_send, b_recv)
 
     loads[0].wait()
-
-    @pl.loop(1, groups)
-    def _(d):
-        p = grp_peer(d)
-        for s in range(S):
-            stage1[p * S + s] = own[tab[t_snd + p * S + s]]
-        f_out(d).start()
-
+    f_post(lambda q, rows: own[tab[t_snd + q], rows], 0, PARTS)
     loads[1].wait()
-
-    @pl.loop(1, groups)
-    def _(d):
-        p = grp_peer(d)
-        for s in range(S):
-            stage2[p * S + s] = past[tab[t_snd + p * S + s]]
-        f_out(d).wait_send()
-        h_out(d).start()
+    h_post(lambda q, rows: past[tab[t_snd + q], rows], 0, PARTS)
 
     loads[3].wait()
 
@@ -160,11 +177,12 @@
         for k in range(K):
             turned[b, pl.ds(k * BLK, BLK), :] = tiles[b, k].T
 
-    loads[2].wait()
+    for load in loads[4:] + loads[2:3]:
+        load.wait()
 
     @pl.loop(1, groups)
     def _(d):
-        f_in(d).wait_recv()
+        f_whole(grp_peer(d)).wait()
 
     def aggregate(table, b):
         wide = jnp.concatenate([tiles[b, k] for k in range(K)], axis=1)
@@ -183,11 +201,18 @@
         table2[blocks] = h.reshape(CHUNK, BLK, D)
         o_hist[rows, :] = h
 
+    keeps = [
+        pltpu.make_async_copy(o_hist, x_hist, load_sem.at[0]),
+        pltpu.make_async_copy(o_hidden, x_hidden, load_sem.at[1]),
+        pltpu.make_async_copy(o_aux, x_aux, load_sem.at[2]),
+        pltpu.make_async_copy(total, x_total, load_sem.at[3]),
+    ]
+    keeps[0].start()
     loss_acc[...] = jnp.zeros((TB, ROWS), F32)
 
     @pl.loop(1, groups)
     def _(d):
-        h_in(d).wait_recv()
+        h_whole(grp_peer(d)).wait_recv()
 
     @pl.loop(0, CHUNKS)
     def _(c):
@@ -219,14 +244,10 @@
                 i = b * K + k
                 chain[i] = spread[k * BLK : (k + 1) * BLK] + chain[tab[t_prev + i]]
 
-    @pl.loop(1, groups)
-    def _(d):
-        p = grp_peer(d)
-        for s in range(S):
-            stage1[p * S + s] = chain[tab[t_last + NB + p * S + s]].astype(BF16)
-        b_out(d).start()
-
-    loads[4].wait()
+    def returned(q, rows):
+        return chain[tab[t_last + NB + q], rows]
+
+    b_post(returned, 0, PARTS // 2)
 
     def put(half, base, value):
         pack[half, :, pl.ds(base, rows_of), :] = (value * scale).reshape(groups, rows_of, D)
@@ -249,6 +270,7 @@
         o_hidden[rows, :] = grad.astype(BF16)
         gp1[rows, :] = (grad * slope(pre1[rows, :])).astype(BF16)
 
+    keeps[1].start()
     put(0, 0, tn(agg1[...], gp1[...]))
     put(1, 0, tn(own[...].reshape(NB * BLK, D), gp1[...]))
 
@@ -257,42 +279,32 @@
         recv_sem=core_sem.at[1], device_id={"clus": sibling}, device_id_type=MESH,
     )
     swap.start()
+
     swap.wait()
     acc[...] = pack[core] + from_core[...]
-
-    def spread_out(d):
-        p = grp_peer(d)
+    narrow[...] = acc[...].astype(BF16)
+
+    def spread_out(p):
         return pltpu.make_async_remote_copy(
-            src_ref=acc.at[p], dst_ref=from_grp.at[g], send_sem=g_send.at[p],
+            src_ref=narrow.at[p], dst_ref=from_grp.at[g], send_sem=g_send.at[p],
             recv_sem=g_recv.at[g], device_id={"grp": p}, device_id_type=MESH,
         )
 
-    @pl.loop(1, groups)
-    def _(d):
-        spread_out(d).start()
+    for p in peers:
+        spread_out(p).start()
+
+    b_post(returned, PARTS // 2, PARTS)
 
     mine[...] = acc[g]
-
-    @pl.loop(1, groups)
-    def _(d):
-        b_in(d).wait_recv()
-
-    @pl.loop(0, slots)
-    def _(i):
-        fold[i] = came[i].astype(F32) + fold[tab[t_qprev + i]]
-
-    @pl.loop(0, NB)
-    def _(j):
-        o_aux[j] = fold[tab[t_qlast + j]].astype(BF16)
 
     @pl.loop(1, groups)
     def _(d):
         p = grp_peer(d)
         pltpu.make_async_remote_copy(
-            src_ref=acc.at[p], dst_ref=from_grp.at[p], send_sem=g_send.at[p],
+            src_ref=narrow.at[p], dst_ref=from_grp.at[p], send_sem=g_send.at[p],
             recv_sem=g_recv.at[p], device_id={"grp": p}, device_id_type=MESH,
         ).wait_recv()
-        mine[...] += from_grp[p]
+        mine[...] += from_grp[p].astype(F32)
 
     def owner(u):
         return (u * depth) // units
@@ -346,10 +358,9 @@
             to_owner(u).wait_send()
             share(u, 1).wait_recv()
 
-    def publish(d, slot):
-        p = grp_peer(d)
+    def publish(p, slot):
         return pltpu.make_async_remote_copy(
-            src_ref=done, dst_ref=total.at[core, slot], send_sem=r_send.at[p],
+            src_ref=final, dst_ref=total.at[core, slot], send_sem=r_send.at[p],
             recv_sem=r_recv.at[slot], device_id={"grp": p}, device_id_type=MESH,
         )
 
@@ -359,40 +370,46 @@
             recv_sem=w_recv.at[p], device_id={"clus": sibling}, device_id_type=MESH,
         )
 
+    final[...] = done[...].astype(BF16)
+
+    for p in peers:
+        publish(p, g).start()
+
+    total[core, g] = final[...]
+    forward(core, g).start()
+
     @pl.loop(1, groups)
     def _(d):
-        publish(d, g).start()
-
-    total[core, g] = done[...]
-    forward(core, g).start()
+        b_whole(grp_peer(d)).wait_recv()
+
+    @pl.loop(0, slots)
+    def _(i):
+        fold[i] = came[i].astype(F32) + fold[tab[t_qprev + i]]
+
+    @pl.loop(0, NB)
+    def _(j):
+        o_aux[pl.ds(j * BLK, BLK), :] = fold[tab[t_qlast + j]].astype(BF16)
+
+    keeps[2].start()
 
     @pl.loop(1, groups)
     def _(d):
         p = grp_peer(d)
-        publish(d, p).wait_recv()
+        publish(p, p).wait_recv()
         forward(core, p).start()
 
     @pl.loop(0, groups)
     def _(p):
         forward(1 - core, p).wait_recv()
 
-    def pick(half, base):
-        return total[half, :, pl.ds(base, rows_of), :].reshape(D, D)
-
-    o_nf[...] = pick(0, 0)
-    o_sf[...] = pick(1, 0)
-    o_ns[...] = pick(0, rows_of)
-    o_ss[...] = pick(1, rows_of)
-    for t in range(TB // 8):
-        o_hz[pl.ds(t * 8, 8), :] = total[t // 2, t % 2, pl.ds(2 * rows_of, 8), :]
-    o_loss[...] = total[0, 2, pl.ds(2 * rows_of, 8), pl.ds(0, LANES)]
+    keeps[3].start()
 
     @pl.loop(1, groups)
     def _(d):
-        h_out(d).wait_send()
-        b_out(d).wait_send()
-        spread_out(d).wait_send()
-        publish(d, g).wait_send()
+        h_whole(grp_peer(d)).wait_send()
+        b_whole(grp_peer(d)).wait_send()
+        spread_out(grp_peer(d)).wait_send()
+        publish(grp_peer(d), g).wait_send()
 
     @pl.loop(0, groups)
     def _(p):
@@ -405,13 +422,58 @@
             def _(d):
                 share(u, d).wait_send()
 
-
-def latest(keys, queries, limits):
-    count = keys.shape[0]
-    place = jnp.arange(count, dtype=jnp.int32)[None, :]
-    hit = (keys[None, :] == queries[:, None]) & (place < limits[:, None])
+    for keep in keeps:
+        keep.wait()
+
+
+def tail_kernel(groups, x_hist, x_hidden, x_aux, x_total,
+                o_hist, o_hidden, o_aux, o_nf, o_sf, o_ns, o_ss, o_hz, o_loss,
+                v_hist, v_hidden, v_aux, total, grads, into, out):
+    rows_of = D // groups
+    first = [
+        pltpu.make_async_copy(a, b, into.at[i])
+        for i, (a, b) in enumerate(
+            ((x_total, total), (x_hist, v_hist), (x_hidden, v_hidden), (x_aux, v_aux))
+        )
+    ]
+    second = [
+        pltpu.make_async_copy(a, b, out.at[i])
+        for i, (a, b) in enumerate(
+            ((v_hist, o_hist), (v_hidden, o_hidden), (v_aux, o_aux), (grads.at[0], o_nf),
+             (grads.at[1], o_sf), (grads.at[2], o_ns), (grads.at[3], o_ss))
+        )
+    ]
+    for copy in first:
+        copy.start()
+    for t in range(1, 4):
+        first[t].wait()
+        second[t - 1].start()
+    first[0].wait()
+    for t, (half, base) in enumerate(((0, 0), (1, 0), (0, rows_of), (1, rows_of))):
+        grads[t] = total[half, :, pl.ds(base, rows_of), :].astype(F32).reshape(D, D)
+        second[3 + t].start()
+    for t in range(TB // 8):
+        o_hz[pl.ds(t * 8, 8), :] = total[t // 2, t % 2, pl.ds(2 * rows_of, 8), :].astype(F32)
+    o_loss[...] = total[0, 2, pl.ds(2 * rows_of, 8), pl.ds(0, LANES)].astype(F32)[0:1, 0:1]
+    for copy in second:
+        copy.wait()
+
+
+def latest(hit):
+    count = hit.shape[1]
+    place = lax.broadcasted_iota(jnp.int32, hit.shape, 1)
     found = jnp.max(jnp.where(hit, place, -1), axis=1)
     return jnp.where(found < 0, count, found)
+
+
+def before(keys):
+    shape = (keys.shape[0], keys.shape[0])
+    earlier = lax.broadcasted_iota(jnp.int32, shape, 1) < lax.broadcasted_iota(jnp.int32, shape, 0)
+    return latest((keys[None, :] == keys[:, None]) & earlier)
+
+
+def holder(keys, count):
+    return latest(keys[None, :] == lax.broadcasted_iota(jnp.int32, (count, keys.shape[0]), 0))
 
 
 def shards(
@@ -427,40 +489,30 @@
     lots = units if depth < units else 1
     src = tile_sources.reshape(TILES)
     snd = send_list.reshape(slots)
-    ints = lambda n: jnp.arange(n, dtype=jnp.int32)
-    full = lambda n, v: jnp.full((n,), v, jnp.int32)
     tab = jnp.concatenate(
         [
-            src,
-            jnp.minimum(snd, NB - 1),
-            latest(
-                src,
-                jnp.concatenate([src, ints(NB + slots)]),
-                jnp.concatenate([ints(TILES), full(NB + slots, TILES)]),
-            ),
-            latest(
-                snd,
-                jnp.concatenate([snd, ints(NB)]),
-                jnp.concatenate([ints(slots), full(NB, slots)]),
-            ),
+            src, jnp.minimum(snd, NB - 1), before(src), holder(src, NB + slots), before(snd),
+            holder(snd, NB),
         ]
     )
     any_spec = pl.BlockSpec(memory_space=pl.ANY)
     vmem = pl.BlockSpec(memory_space=pltpu.VMEM)
     dma = pltpu.SemaphoreType.DMA
     nodes = NB * BLK
-    out_shape = (
-        jax.ShapeDtypeStruct((nodes, D), BF16),
-        jax.ShapeDtypeStruct((nodes, D), BF16),
-        jax.ShapeDtypeStruct((NB, BLK, D), BF16),
-        jax.ShapeDtypeStruct((D, D), F32),
-        jax.ShapeDtypeStruct((D, D), F32),
-        jax.ShapeDtypeStruct((D, D), F32),
-        jax.ShapeDtypeStruct((D, D), F32),
-        jax.ShapeDtypeStruct((TB, D), F32),
-        jax.ShapeDtypeStruct((8, LANES), F32),
-    )
+    nodes_out = jax.ShapeDtypeStruct((nodes, D), BF16)
+    weight_out = jax.ShapeDtypeStruct((D, D), F32)
+    total_out = jax.ShapeDtypeStruct((2, groups, piece, D), BF16)
     scratch = [
+        pltpu.VMEM((nodes, D), BF16),
+        pltpu.VMEM((nodes, D), BF16),
+        pltpu.VMEM((nodes, D), BF16),
+        pltpu.VMEM((CHUNKS, 1, ROWS), jnp.int32),
+        pltpu.VMEM((CHUNKS, 1, ROWS), jnp.int32),
+        pltpu.VMEM((D, D), BF16),
+        pltpu.VMEM((D, D), BF16),
+        pltpu.VMEM((D, D), BF16),
+        pltpu.VMEM((D, D), BF16),
+        pltpu.VMEM((TB, D), BF16),
         pltpu.VMEM((NB, BLK, D), BF16),
         pltpu.VMEM((NB, BLK, D), BF16),
         pltpu.VMEM((nodes, D), BF16),
@@ -482,14 +534,16 @@
         pltpu.VMEM((slots + 1, BLK, D), F32),
         pltpu.VMEM((TB, ROWS), F32),
         pltpu.VMEM((2, groups, piece, D), F32),
-        pltpu.VMEM((2, groups, piece, D), F32),
+        pltpu.VMEM((2, groups, piece, D), BF16),
         pltpu.VMEM((groups, piece, D), F32),
+        pltpu.VMEM((groups, piece, D), BF16),
         pltpu.VMEM((groups, piece, D), F32),
-        pltpu.VMEM((groups, piece, D), F32),
+        pltpu.VMEM((groups, piece, D), BF16),
         pltpu.VMEM((piece, D), F32),
         pltpu.VMEM((lots, depth, 8, LANES), F32),
         pltpu.VMEM((piece, D), F32),
-        dma((5,)),
+        pltpu.VMEM((piece, D), BF16),
+        dma((12,)),
         dma((groups,)), dma((groups,)), dma((groups,)), dma((groups,)), dma((groups,)),
         dma((groups,)),
         dma((2,)), dma((groups,)), dma((groups,)), dma((units,)), dma((lots, depth)),
@@ -498,9 +552,9 @@
     ]
     outs = pl.pallas_call(
         functools.partial(program_kernel, groups, depth),
-        out_shape=out_shape,
-        in_specs=[pl.BlockSpec(memory_space=pltpu.SMEM)] + [any_spec] * 4 + [vmem] * 7,
-        out_specs=(vmem,) * 9,
+        out_shape=(nodes_out,) * 3 + (total_out,),
+        in_specs=[pl.BlockSpec(memory_space=pltpu.SMEM)] + [any_spec] * 11,
+        out_specs=(any_spec,) * 4,
         scratch_shapes=scratch,
         compiler_params=pltpu.CompilerParams(
             collective_id=0, has_side_effects=True, vmem_limit_bytes=56 << 20
@@ -515,9 +569,26 @@
         event_flags.reshape(CHUNKS, 1, ROWS),
         neigh_first, self_first, neigh_second, self_second, hazard_weight.T,
     )
-    hist, hidden, aux, nf, sf, ns, ss, hz, loss = outs
+    hist, hidden, aux, nf, sf, ns, ss, hz, loss = pl.pallas_call(
+        functools.partial(tail_kernel, groups),
+        out_shape=(nodes_out,) * 3 + (weight_out,) * 4 + (
+            jax.ShapeDtypeStruct((TB, D), F32), jax.ShapeDtypeStruct((1, 1), F32),
+        ),
+        in_specs=[any_spec] * 4,
+        out_specs=(any_spec,) * 7 + (vmem,) * 2,
+        scratch_shapes=[
+            pltpu.VMEM((nodes, D), BF16),
+            pltpu.VMEM((nodes, D), BF16),
+            pltpu.VMEM((nodes, D), BF16),
+            pltpu.VMEM((2, groups, piece, D), BF16),
+            pltpu.VMEM((4, D, D), F32),
+            dma((4,)),
+            dma((7,)),
+        ],
+        compiler_params=pltpu.CompilerParams(vmem_limit_bytes=58 << 20),
+    )(*outs)
     return (
-        hist[None, None], hidden[None, None], aux.reshape(1, 1, nodes, D),
+        hist[None, None], hidden[None, None], aux[None, None],
         nf, sf, ns, ss, hz.T, loss[0, 0],
     )
 

time: 168 us -> 125 us (0.74)
  Pallas kernels: 153 us -> 121 us
  local copies, waits for them, and re-layouts: 12.8 us -> 2.15 us
    pallas_call x1, Pallas kernels: 153 us -> 118 us  [shards(): pl.pallas_call(functools.partial(program_kernel, groups, depth), out_shap...]
    unnamed x32 -> x6, local copies, waits for them, and re-layouts: 11.4 us -> 1.33 us
    pallas_call x0 -> x1, Pallas kernels: none -> 3.43 us  [shards(): pl.pallas_call(functools.partial(tail_kernel, groups), out_shape=(nodes_o...]
where the time goes in v3:
time: 125 us
  Pallas kernels  121 us (97%)
  local copies, waits for them, and re-layouts  2.15 us (2%)
    pallas_call x1, Pallas kernels, shards(): pl.pallas_call(functools.partial(program_kernel, groups, depth), out_shap...  118 us
    pallas_call x1, Pallas kernels, shards(): pl.pallas_call(functools.partial(tail_kernel, groups), out_shape=(nodes_o...  3.43 us

profile of v3, /device:TPU:1, one launch (start us, length us, event | category | flops | bytes accessed | tf_op | source)
XLA Modules:
  0.0 124.7 jit_solution(17915652038289167701)
XLA Ops:
  0.6 0.0 copy-start
  0.7 0.7 copy-done
  1.3 0.1 copy.26
  1.4 0.1 reshape.46
  1.5 0.1 select_reduce_fusion.1
  1.6 0.0 copy-start.1
  1.6 0.2 select_reduce_fusion.2
  1.8 0.5 copy-done.1
  2.3 0.1 copy.27
  2.4 0.1 reshape.47
  2.4 0.1 select_reduce_fusion.3
  2.6 0.2 select_reduce_fusion
  2.8 0.6 concatenate.3.tab
  3.4 117.8 %shard_map.196 = (bf16[1024,256]{1,0:T(8,128)(2,1)}, bf16[1024,256]{1,0:T(8,128)(2,1)}, bf16[1024,256]{1,0:T(8,128)(2,1)}, bf16[2,16,40,256]{3,2,1,0:T(8,128)(2,1)}) custom-call(s32[176]{0:T(256)} %concatenate.3.tab, bf16[8,128,256]{2,1,0:T(8,128)(2,1)} %bitcast.17, bf16[8,128,256]{2,1,0:T(8,128)(2,1)} %bitcast.18, bf16[1024,256]{1,0:T(8,128)(2,1)} %bitcast.19, ...), custom_call_target="tpu_custom_call" | custom-call | tf_op jit(solution)/shard_map/pallas_call | solution.py:553
  121.2 3.4 %shard_map.197 = (bf16[1024,256]{1,0:T(8,128)(2,1)}, bf16[1024,256]{1,0:T(8,128)(2,1)}, bf16[1024,256]{1,0:T(8,128)(2,1)}, f32[256,256]{1,0:T(8,128)}, f32[256,2...) custom-call(bf16[1024,256]{1,0:T(8,128)(2,1)} %get-tuple-element.22.x_hist, ...), custom_call_target="tpu_custom_call" | custom-call | tf_op jit(solution)/shard_map/pallas_call | solution.py:572
  (4 shorter events, 0.0 us)
Async XLA Ops:
  0.6 0.7 copy-start
  1.6 0.7 copy-start.1

commit v4 on v3

--- a/solution.py
+++ b/solution.py
@@ -247,7 +247,7 @@
     def returned(q, rows):
         return chain[tab[t_last + NB + q], rows]
 
-    b_post(returned, 0, PARTS // 2)
+    b_post(returned, 0, PARTS // 4)
 
     def put(half, base, value):
         pack[half, :, pl.ds(base, rows_of), :] = (value * scale).reshape(groups, rows_of, D)
@@ -293,7 +293,7 @@
     for p in peers:
         spread_out(p).start()
 
-    b_post(returned, PARTS // 2, PARTS)
+    b_post(returned, PARTS // 4, PARTS)
 
     mine[...] = acc[g]
 

time: 125 us -> 117 us (0.936)
  Pallas kernels: 121 us -> 113 us
    pallas_call x1, Pallas kernels: 118 us -> 110 us  [shards(): pl.pallas_call(functools.partial(program_kernel, groups, depth), out_shap...]
where the time goes in v4:
time: 117 us
  Pallas kernels  113 us (97%)
  local copies, waits for them, and re-layouts  2.15 us (2%)
    pallas_call x1, Pallas kernels, shards(): pl.pallas_call(functools.partial(program_kernel, groups, depth), out_shap...  110 us
    pallas_call x1, Pallas kernels, shards(): pl.pallas_call(functools.partial(tail_kernel, groups), out_shape=(nodes_o...  3.43 us

profile of v4, /device:TPU:1, one launch (start us, length us, event | category | flops | bytes accessed | tf_op | source)
XLA Modules:
  0.0 116.9 jit_solution(17262098980107615745)
XLA Ops:
  0.6 0.0 copy-start
  0.7 0.7 copy-done
  1.3 0.1 copy.26
  1.4 0.1 reshape.46
  1.5 0.1 select_reduce_fusion.1
  1.6 0.0 copy-start.1
  1.6 0.2 select_reduce_fusion.2
  1.8 0.5 copy-done.1
  2.3 0.1 copy.27
  2.4 0.1 reshape.47
  2.4 0.1 select_reduce_fusion.3
  2.6 0.2 select_reduce_fusion
  2.8 0.6 concatenate.3.tab
  3.4 110.0 %shard_map.196 = (bf16[1024,256]{1,0:T(8,128)(2,1)}, bf16[1024,256]{1,0:T(8,128)(2,1)}, bf16[1024,256]{1,0:T(8,128)(2,1)}, bf16[2,16,40,256]{3,2,1,0:T(8,128)(2,1)}) custom-call(s32[176]{0:T(256)} %concatenate.3.tab, bf16[8,128,256]{2,1,0:T(8,128)(2,1)} %bitcast.17, bf16[8,128,256]{2,1,0:T(8,128)(2,1)} %bitcast.18, bf16[1024,256]{1,0:T(8,128)(2,1)} %bitcast.19, ...), custom_call_target="tpu_custom_call" | custom-call | tf_op jit(solution)/shard_map/pallas_call | solution.py:553
  113.5 3.4 %shard_map.197 = (bf16[1024,256]{1,0:T(8,128)(2,1)}, bf16[1024,256]{1,0:T(8,128)(2,1)}, bf16[1024,256]{1,0:T(8,128)(2,1)}, f32[256,256]{1,0:T(8,128)}, f32[256,2...) custom-call(bf16[1024,256]{1,0:T(8,128)(2,1)} %get-tuple-element.22.x_hist, ...), custom_call_target="tpu_custom_call" | custom-call | tf_op jit(solution)/shard_map/pallas_call | solution.py:572
  (4 shorter events, 0.0 us)
Async XLA Ops:
  0.6 0.7 copy-start
  1.6 0.7 copy-start.1

commit v5 on v4

--- a/solution.py
+++ b/solution.py
@@ -293,7 +293,7 @@
     for p in peers:
         spread_out(p).start()
 
-    b_post(returned, PARTS // 4, PARTS)
+    b_post(returned, PARTS // 4, 3)
 
     mine[...] = acc[g]
 
@@ -375,6 +375,7 @@
     for p in peers:
         publish(p, g).start()
 
+    b_post(returned, 3, PARTS)
     total[core, g] = final[...]
     forward(core, g).start()
 

time: 117 us -> 122 us (1.043)
  Pallas kernels: 113 us -> 118 us
    pallas_call x1, Pallas kernels: 110 us -> 115 us  [shards(): pl.pallas_call(functools.partial(program_kernel, groups, depth), out_shap...]
where the time goes in v5:
time: 122 us
  Pallas kernels  118 us (97%)
  local copies, waits for them, and re-layouts  2.15 us (2%)
    pallas_call x1, Pallas kernels, shards(): pl.pallas_call(functools.partial(program_kernel, groups, depth), out_shap...  115 us
    pallas_call x1, Pallas kernels, shards(): pl.pallas_call(functools.partial(tail_kernel, groups), out_shape=(nodes_o...  3.43 us

profile of v5, /device:TPU:1, one launch (start us, length us, event | category | flops | bytes accessed | tf_op | source)
XLA Modules:
  0.0 121.7 jit_solution(3947620665235961423)
XLA Ops:
  0.6 0.0 copy-start
  0.7 0.7 copy-done
  1.3 0.1 copy.26
  1.4 0.1 reshape.46
  1.5 0.1 select_reduce_fusion.1
  1.6 0.0 copy-start.1
  1.6 0.2 select_reduce_fusion.2
  1.8 0.5 copy-done.1
  2.3 0.1 copy.27
  2.4 0.1 reshape.47
  2.4 0.1 select_reduce_fusion.3
  2.6 0.2 select_reduce_fusion
  2.8 0.6 concatenate.3.tab
  3.4 114.8 %shard_map.196 = (bf16[1024,256]{1,0:T(8,128)(2,1)}, bf16[1024,256]{1,0:T(8,128)(2,1)}, bf16[1024,256]{1,0:T(8,128)(2,1)}, bf16[2,16,40,256]{3,2,1,0:T(8,128)(2,1)}) custom-call(s32[176]{0:T(256)} %concatenate.3.tab, bf16[8,128,256]{2,1,0:T(8,128)(2,1)} %bitcast.17, bf16[8,128,256]{2,1,0:T(8,128)(2,1)} %bitcast.18, bf16[1024,256]{1,0:T(8,128)(2,1)} %bitcast.19, ...), custom_call_target="tpu_custom_call" | custom-call | tf_op jit(solution)/shard_map/pallas_call | solution.py:554
  118.3 3.4 %shard_map.197 = (bf16[1024,256]{1,0:T(8,128)(2,1)}, bf16[1024,256]{1,0:T(8,128)(2,1)}, bf16[1024,256]{1,0:T(8,128)(2,1)}, f32[256,256]{1,0:T(8,128)}, f32[256,2...) custom-call(bf16[1024,256]{1,0:T(8,128)(2,1)} %get-tuple-element.22.x_hist, ...), custom_call_target="tpu_custom_call" | custom-call | tf_op jit(solution)/shard_map/pallas_call | solution.py:573
  (4 shorter events, 0.0 us)
Async XLA Ops:
  0.6 0.7 copy-start
  1.6 0.7 copy-start.1
